TPU v7x, 32 devices: a whole 2x2x4 slice. The times are simulated.
32 devices in a mesh: grp: 2 (over y), pre: 4 (over z), stg: 2 (over x), tp: 2 (over core).
Axes of the slice: x: 2, y: 2, z: 4, core: 2. Of those that a mesh axis runs over, the one named last changes fastest.
Arguments:
- queries: bfloat16 [32, 256, 4096], P(('grp', 'pre'), 'stg', 'tp'), parts along dimension 0, may hold values from -6 to 6
- doc_keys: bfloat16 [32, 256, 512], P(('grp', 'pre'), 'stg', 'tp'), parts along dimension 0, may hold values from -6 to 6
- doc_values: bfloat16 [32, 256, 512], P(('grp', 'pre'), 'stg', 'tp'), parts along dimension 0, may hold values from -48 to 48
- prefix_keys: bfloat16 [8, 1024, 512], P(('grp', 'pre'), None, 'tp'), parts along dimension 0, may hold values from -6 to 6
- prefix_values: bfloat16 [8, 1024, 512], P(('grp', 'pre'), None, 'tp'), parts along dimension 0, may hold values from -48 to 48
- template: int32 [32, 1], P(('grp', 'pre')), parts along dimension 0, may hold values from 0 to 3; in each aligned block of 4 rows (0 to 3, 4 to 7, ...) no two rows name the same one
- owner_table: int32 [8], P('grp'), parts along dimension 0, may hold values from 0 to 3, each once
Outputs:
- attended: bfloat16 [32, 256, 4096], P(('grp', 'pre'), 'stg', 'tp'), parts along dimension 0
There are 2 independent parts, one for each index of `grp`. A program takes and returns all parts, laid end to end along the dimension named above; each array names one. Nothing has to cross between parts.
Inputs may be any that keep to these rules, and one draw needn't show every extreme that they name: No template is named by more than one of the 4 documents of one index of pre. `owner_table`: each owner holds the cache of exactly one template.
All inputs are finite; a program needn't handle non-finite values.
Results may differ from a plain program's by a relative error of at most 0.0034.
Values may be sent and summed in bfloat16 or wider, within the bound.
No kernel may reach another device: no remote copies, remote signals or barrier semaphores. Data moves between devices by JAX's collectives and lax.ppermute only.
A program may use at most 128 MiB of HBM per device.

v0:
```python
import jax
import jax.numpy as jnp
from jax import lax
from jax.sharding import PartitionSpec as P

H = 32
KVH = 4
HD = 128


def prefix_part(rows_in, cache_keys, cache_values, kv_local):
    row_count = rows_in.shape[0]
    groups = H // KVH
    length = cache_keys.shape[0]
    query_heads = rows_in.reshape(row_count, kv_local, groups, HD)
    key_heads = cache_keys.reshape(length, kv_local, HD)
    value_heads = cache_values.reshape(length, kv_local, HD)
    scores = jnp.einsum(
        "tkgh,skh->kgts", query_heads, key_heads, preferred_element_type=jnp.float32
    ) * HD ** (-0.5)
    highest = jnp.max(scores, axis=-1, keepdims=True)
    weights = jnp.exp(scores - highest)
    totals = jnp.sum(weights, axis=-1)
    summed = jnp.einsum(
        "kgts,skh->tkgh",
        weights.astype(jnp.bfloat16),
        value_heads,
        preferred_element_type=jnp.float32,
    )
    output = summed / jnp.transpose(totals, (2, 0, 1))[..., None]
    log_total = jnp.transpose(highest[..., 0] + jnp.log(totals), (2, 0, 1))
    return (
        output.reshape(row_count, kv_local * groups * HD).astype(jnp.bfloat16),
        log_total.reshape(row_count, kv_local * groups),
    )


def shards(queries, doc_keys, doc_values, prefix_keys, prefix_values, template, owner_table):
    kv_local = KVH // lax.axis_size("tp")
    groups = H // KVH
    docs_here, span_len, features = queries.shape
    templates_all = owner_table.shape[0]
    matches = template == jnp.arange(templates_all, dtype=jnp.int32)[None, :]
    holders = jnp.sum(jnp.where(matches, owner_table[None, :], 0), axis=1)
    whole_keys, whole_values = (
        lax.all_gather(prefix_keys, "pre", axis=0, tiled=True),
        lax.all_gather(prefix_values, "pre", axis=0, tiled=True),
    )

    def per_document(packed):
        doc_rows, holder = packed
        cache_keys = lax.dynamic_index_in_dim(whole_keys, holder, 0, keepdims=False)
        cache_values = lax.dynamic_index_in_dim(whole_values, holder, 0, keepdims=False)
        return prefix_part(doc_rows, cache_keys, cache_values, kv_local)

    prefix_rounded, prefix_log = lax.map(per_document, (queries, holders))
    prefix_out = prefix_rounded.astype(jnp.float32)
    query_heads = queries.reshape(docs_here, span_len, kv_local, groups, HD)
    query_pos = lax.axis_index("stg") * span_len + jnp.arange(span_len, dtype=jnp.int32)
    running_max = jnp.full((docs_here, kv_local, groups, span_len), -1e30, jnp.float32)
    key_piece = lax.all_gather(doc_keys, "stg", axis=1, tiled=True)
    value_piece = lax.all_gather(doc_values, "stg", axis=1, tiled=True)
    piece_len = key_piece.shape[1]
    key_heads = key_piece.reshape(docs_here, piece_len, kv_local, HD)
    value_heads = value_piece.reshape(docs_here, piece_len, kv_local, HD)
    scores = jnp.einsum(
        "dtkgh,dskh->dkgts", query_heads, key_heads, preferred_element_type=jnp.float32
    ) * HD ** (-0.5)
    key_pos = jnp.arange(piece_len, dtype=jnp.int32)
    visible = query_pos[:, None] >= key_pos[None, :]
    scores = jnp.where(visible, scores, -1e30)
    new_max = jnp.maximum(running_max, jnp.max(scores, axis=-1))
    weights = jnp.where(visible, jnp.exp(scores - new_max[..., None]), 0.0)
    new_sum = jnp.sum(weights, axis=-1)
    added = jnp.einsum(
        "dkgts,dskh->dkgth",
        weights.astype(jnp.bfloat16),
        value_heads,
        preferred_element_type=jnp.float32,
    )
    local_heads = jnp.transpose(added / new_sum[..., None], (0, 3, 1, 2, 4))
    local_log = jnp.transpose(new_max + jnp.log(new_sum), (0, 3, 1, 2))
    prefix_heads = prefix_out.reshape(docs_here, span_len, kv_local, groups, HD)
    prefix_log = prefix_log.reshape(docs_here, span_len, kv_local, groups)
    joint_log = jnp.logaddexp(prefix_log, local_log)
    mixture = (
        jnp.exp(prefix_log - joint_log)[..., None] * prefix_heads
        + jnp.exp(local_log - joint_log)[..., None] * local_heads
    )
    return mixture.reshape(docs_here, span_len, features).astype(jnp.bfloat16)


def solution(mesh):
    return jax.shard_map(
        shards,
        mesh=mesh,
        in_specs=(
            P(("grp", "pre"), "stg", "tp"),
            P(("grp", "pre"), "stg", "tp"),
            P(("grp", "pre"), "stg", "tp"),
            P(("grp", "pre"), None, "tp"),
            P(("grp", "pre"), None, "tp"),
            P(("grp", "pre"), None),
            P("grp"),
        ),
        out_specs=P(("grp", "pre"), "stg", "tp"),
        check_vma=False,
    )
```

profile of v0, /device:TPU:0, one launch (start us, length us, event | category | flops | bytes accessed | tf_op | source)
XLA Modules:
  0.0 162.4 jit_solution(14893409723854206342)
XLA Ops:
  6.5 0.7 all-gather.3.cloned.1.call-update
  7.3 0.7 all-gather.5.cloned.1.call-update
  8.0 1.1 copy.44
  9.2 2.2 %copy.64 = bf16[64,8,16,128]{3,2,1,0:T(8,128)(2,1)S(1)} copy(bf16[64,8,16,128]{3,1,2,0:T(8,128)(2,1)} %bitcast.145) | data formatting | bytes 4194304
  11.4 10.2 %all_gather.15 = bf16[4,256,256]{2,1,0:T(8,128)(2,1)S(1)} all-gather(bf16[4,128,256]{2,1,0:T(8,128)(2,1)} %param.11), channel_id=1, replica_groups=mesh['grp'=2,'pre'=4,'stg'=2,'tp'=2] {'stg'}, dimensions={1}, use_global_device_ids=true | all-gather | bytes 786432 | tf_op jit(solution)/shard_map/all_gather | solution.py:62
  21.8 0.9 select_reduce_fusion
  22.6 8.2 %all_gather.14 = bf16[4,256,256]{1,2,0:T(8,128)(2,1)S(1)} all-gather(bf16[4,128,256]{1,2,0:T(8,128)(2,1)S(1)} %copy.44), channel_id=1, replica_groups=mesh['grp'=2,'pre'=4,'stg'=2,'tp'=2] {'stg'}, dimensions={1}, use_global_device_ids=true | all-gather | bytes 786432 | tf_op jit(solution)/shard_map/all_gather | solution.py:61
  30.8 1.8 %fusion.13 = (f32[4,2,8,128]{3,2,1,0:T(8,128)S(1)}, f32[4,2,256,128,8]{3,2,4,1,0:T(8,128)S(1)}) fusion(pred[128,256]{0,1:T(8,128)(4,1)S(1)} %iota_compare_fusion, bf16[4,256,2,128,1]{1,3,4,2,0:T(8,128)(2,1)S(1)} %bitcast.148, bf16[4,128,2,8,128]{4,3,2,1,0:T(8,128)(2,1)S(1)} %bitcast.146), kind=kOutput, calls=%fused_computation.19 | convolution fusion | flops 543154176 | bytes 11075584 | tf_op jit(solution)/shard_map/dtkgh,dskh->dkgts/dot_general | solution.py:66
  32.7 3.2 %copy-done = f32[4,2,256,128,8]{3,2,4,1,0:T(8,128)} copy-done((f32[4,2,256,128,8]{3,2,4,1,0:T(8,128)}, f32[4,2,256,128,8]{3,2,4,1,0:T(8,128)S(1)}, u32[]{:S(2)}) %copy-start) | copy-done | bytes 8388632
  35.9 2.1 %fusion.15 = f32[4,2,8,128]{3,2,1,0:T(8,128)S(1)} fusion(f32[4,2,256,128,8]{3,2,4,1,0:T(8,128)S(1)} %get-tuple-element.87, f32[4,2,8,128]{3,2,1,0:T(8,128)S(1)} %broadcast_maximum_fusion, pred[128,256]{0,1:T(8,128)(4,1)S(1)} %iota_compare_fusion), kind=kLoop, calls=%fused_computation.21 | loop fusion | flops 10477568 | bytes 8486912 | tf_op jit(solution)/shard_map/reduce_sum | solution.py:74
  37.9 19.4 %all-gather.3.cloned.1.call-done = bf16[4,1024,256]{2,1,0:T(8,128)(2,1)} async-done(((bf16[1,1024,256]{2,1,0:T(8,128)(2,1)}), bf16[4,1024,256]{2,1,0:T(8,128)(2,1)}) %all-gather.3.cloned.1.call-update) | async-done | bytes 2097168 | tf_op jit(solution)/shard_map/all_gather | solution.py:47
  57.3 46.1 %all-gather.5.cloned.1.call-done = bf16[4,1024,256]{2,1,0:T(8,128)(2,1)} async-done(((bf16[1,1024,256]{2,1,0:T(8,128)(2,1)}), bf16[4,1024,256]{2,1,0:T(8,128)(2,1)}) %all-gather.5.cloned.1.call-update) | async-done | bytes 2097168 | tf_op jit(solution)/shard_map/all_gather | solution.py:46
  103.4 42.8 %while.12 = (s32[]{:T(128)}, bf16[4,128,2048]{1,2,0:T(8,128)(2,1)}, f32[4,128,16]{1,2,0:T(8,128)S(1)}, s32[4]{0:T(128)S(1)}, bf16[4,1024,256]{2,1,0:T(8,128)(2,1...) while((s32[]{:T(128)}, bf16[4,128,2048]{1,2,0:T(8,128)(2,1)}, ...), condition=%wide.region_4.5_spmd, body=%wide.region_1.4_spmd.sunk | while | flops 1091041280 | bytes 34668712 | solution.py:56
  103.4 0.6 dynamic_slice.23
  105.8 1.3 constant_dynamic-slice_fusion.5
  107.3 0.2 copy.73
  107.5 1.1 constant_dynamic-slice_fusion.6
  108.6 0.3 copy.74
  108.9 1.3 bitcast_reduce_fusion.2
  110.2 1.4 fusion.50
  111.6 1.7 %divide_convert_fusion.2 = bf16[128,2,8,128]{0,3,2,1:T(8,128)(2,1)S(1)} fusion(bf16[1024,2,128,1]{0,2,3,1:T(8,128)(2,1)S(1)} %bitcast.143, f32[2,1024,128,8]{2,1,3,0:T(8,128)S(1)} %get-tuple-element.137, f32[2,8,128]{2,1,0:T(8,128)S(1)} %get-tuple-element.138, f32[128,2,8]{0,2,1:T(8,128)S(1)} %bitcast.149), kind=kOutput, calls=%fused_computation.9.clone.1 | convolution fusion | flops 543686656 | bytes 9453568 | tf_op jit(solution)/shard_map/while/body/eval_jaxpr/kgts,skh->tkgh/dot_general | solution.py:24
  113.2 0.8 constant_dynamic-update-slice_fusion.2
  114.1 0.6 dynamic_slice.23
  116.5 1.3 constant_dynamic-slice_fusion.5
  118.2 1.1 constant_dynamic-slice_fusion.6
  119.3 0.3 copy.74
  119.6 1.3 bitcast_reduce_fusion.2
  120.9 1.4 fusion.50
  122.3 1.7 %divide_convert_fusion.2 = bf16[128,2,8,128]{0,3,2,1:T(8,128)(2,1)S(1)} fusion(bf16[1024,2,128,1]{0,2,3,1:T(8,128)(2,1)S(1)} %bitcast.143, f32[2,1024,128,8]{2,1,3,0:T(8,128)S(1)} %get-tuple-element.137, f32[2,8,128]{2,1,0:T(8,128)S(1)} %get-tuple-element.138, f32[128,2,8]{0,2,1:T(8,128)S(1)} %bitcast.149), kind=kOutput, calls=%fused_computation.9.clone.1 | convolution fusion | flops 543686656 | bytes 9453568 | tf_op jit(solution)/shard_map/while/body/eval_jaxpr/kgts,skh->tkgh/dot_general | solution.py:24
  124.0 0.8 constant_dynamic-update-slice_fusion.2
  124.8 0.6 dynamic_slice.23
  127.2 1.3 constant_dynamic-slice_fusion.5
  128.9 1.1 constant_dynamic-slice_fusion.6
  130.0 0.3 copy.74
  130.3 1.3 bitcast_reduce_fusion.2
  131.6 1.4 fusion.50
  133.0 1.7 %divide_convert_fusion.2 = bf16[128,2,8,128]{0,3,2,1:T(8,128)(2,1)S(1)} fusion(bf16[1024,2,128,1]{0,2,3,1:T(8,128)(2,1)S(1)} %bitcast.143, f32[2,1024,128,8]{2,1,3,0:T(8,128)S(1)} %get-tuple-element.137, f32[2,8,128]{2,1,0:T(8,128)S(1)} %get-tuple-element.138, f32[128,2,8]{0,2,1:T(8,128)S(1)} %bitcast.149), kind=kOutput, calls=%fused_computation.9.clone.1 | convolution fusion | flops 543686656 | bytes 9453568 | tf_op jit(solution)/shard_map/while/body/eval_jaxpr/kgts,skh->tkgh/dot_general | solution.py:24
  134.7 0.8 constant_dynamic-update-slice_fusion.2
  135.5 0.6 dynamic_slice.23
  137.9 1.3 constant_dynamic-slice_fusion.5
  139.6 1.1 constant_dynamic-slice_fusion.6
  140.7 0.3 copy.74
  141.0 1.3 bitcast_reduce_fusion.2
  142.3 1.4 fusion.50
  143.7 1.7 %divide_convert_fusion.2 = bf16[128,2,8,128]{0,3,2,1:T(8,128)(2,1)S(1)} fusion(bf16[1024,2,128,1]{0,2,3,1:T(8,128)(2,1)S(1)} %bitcast.143, f32[2,1024,128,8]{2,1,3,0:T(8,128)S(1)} %get-tuple-element.137, f32[2,8,128]{2,1,0:T(8,128)S(1)} %get-tuple-element.138, f32[128,2,8]{0,2,1:T(8,128)S(1)} %bitcast.149), kind=kOutput, calls=%fused_computation.9.clone.1 | convolution fusion | flops 543686656 | bytes 9453568 | tf_op jit(solution)/shard_map/while/body/eval_jaxpr/kgts,skh->tkgh/dot_general | solution.py:24
  145.4 0.8 constant_dynamic-update-slice_fusion.2
  146.3 6.7 %fusion.19 = bf16[4,128,2,8,128]{1,4,3,2,0:T(8,128)(2,1)S(1)} fusion(bf16[4,128,2,8,128]{1,4,3,2,0:T(8,128)(2,1)} %bitcast.152, f32[4,128,2,8]{1,3,2,0:T(8,128)S(1)} %bitcast.151, f32[4,128,2,8]{1,3,2,0:T(8,128)S(1)} %get-tuple-element.85, f32[4,128,2,8]{1,3,2,0:T(8,128)S(1)} %get-tuple-element.84, bf16[4,256,2,128,1]{1,3,4,2,0:T(8,128)(2,1)S(1)} %bitcast.150, ...), kind=kOutput, calls=%fused_computation.25 | convolution fusion | flops 553648128 | bytes 13271040 | tf_op jit(solution)/shard_map/dkgts,dskh->dkgth/dot_general | solution.py:75
  152.9 2.6 %copy.49 = bf16[4,128,2048]{2,1,0:T(8,128)(2,1)} copy(bf16[4,128,2048]{1,2,0:T(8,128)(2,1)S(1)} %bitcast.147) | data formatting | bytes 4194304 | tf_op jit(solution)/shard_map/convert_element_type | solution.py:90
  (21 shorter events, 1.8 us)
Async XLA Ops:
  6.5 50.8 %all-gather.3.cloned.1.call-start = ((), (), s32[]{:S(2)}) async-start(), calls=%async_computation | async-start | bytes 2621440 | tf_op jit(solution)/shard_map/all_gather | solution.py:47
  7.3 96.1 %all-gather.5.cloned.1.call-start = ((), (), s32[]{:S(2)}) async-start(), calls=%async_computation.1 | async-start | bytes 2621440 | tf_op jit(solution)/shard_map/all_gather | solution.py:46
  32.6 3.2 %copy-start = (f32[4,2,256,128,8]{3,2,4,1,0:T(8,128)}, f32[4,2,256,128,8]{3,2,4,1,0:T(8,128)S(1)}, u32[]{:S(2)}) copy-start(f32[4,2,256,128,8]{3,2,4,1,0:T(8,128)S(1)} %get-tuple-element.87) | copy-start | bytes 25165828
Sparse Core Ops, SparseCore 0:
  8.9 48.3 all-gather.2
  58.9 44.4 all-gather.4
where the time goes:
time: 163 us; the launch traced here: 162 us
  waiting for transfers between devices  66.8 us (41%)
  local copies, waits for them, and re-layouts  27.3 us (17%)
  matrix products  20.4 us (13%)
  blocking collectives  18.4 us (11%)
  between operations  13.5 us (8%)
  other arithmetic  8.5 us (5%)
  loops' own time  7.46 us (5%)
    all_gather x1, waiting for transfers between devices, shards(): lax.all_gather(prefix_keys, 'pre', axis=0, tiled=True)  46.1 us
    all_gather x1, waiting for transfers between devices, shards(): lax.all_gather(prefix_values, 'pre', axis=0, tiled=True)  19.4 us
    all_gather x1, blocking collectives, shards(): value_piece = lax.all_gather(doc_values, 'stg', axis=1, tiled=True)  10.2 us
    all_gather x1, blocking collectives, shards(): key_piece = lax.all_gather(doc_keys, 'stg', axis=1, tiled=True)  8.17 us
    dynamic_slice x12, local copies, waits for them, and re-layouts, shards(): prefix_rounded, prefix_log = lax.map(per_document, (queries, holders))  7.86 us
    another operation x1, loops' own time, shards(): prefix_rounded, prefix_log = lax.map(per_document, (queries, holders))  7.46 us
    dot_general x4, matrix products, prefix_part(): jnp.einsum('kgts,skh->tkgh', weights.astype(jnp.bfloat16), value_heads, p...  6.72 us
    dot_general x1, matrix products, shards(): jnp.einsum('dkgts,dskh->dkgth', weights.astype(jnp.bfloat16), value_heads...  6.67 us
  transfers between devices with their start and end apart: 2, of which 2 were waited for; matrix products, arithmetic and copies ran while one was open for 5% of the time, Pallas kernels for 0%

commit v1 on v0

--- a/solution.py
+++ b/solution.py
@@ -1,11 +1,22 @@
+import functools
+import math
+
 import jax
 import jax.numpy as jnp
 from jax import lax
+from jax.experimental import pallas as pl
+from jax.experimental.pallas import tpu as pltpu
 from jax.sharding import PartitionSpec as P
 
 H = 32
 KVH = 4
 HD = 128
+GROUPS = H // KVH
+STACK = 2
+LOG2_SCALE = HD**-0.5 * math.log2(math.e)
+HIDDEN = -1e30
+ROWS_BY_FEATURES = (((1,), (1,)), ((), ()))
+ROWS_BY_KEYS = (((1,), (0,)), ((), ()))
 
 
 def prefix_part(rows_in, cache_keys, cache_values, kv_local):
@@ -35,13 +46,10 @@
     )
 
 
-def shards(queries, doc_keys, doc_values, prefix_keys, prefix_values, template, owner_table):
+def gathered(queries, doc_keys, doc_values, prefix_keys, prefix_values, holders):
     kv_local = KVH // lax.axis_size("tp")
     groups = H // KVH
     docs_here, span_len, features = queries.shape
-    templates_all = owner_table.shape[0]
-    matches = template == jnp.arange(templates_all, dtype=jnp.int32)[None, :]
-    holders = jnp.sum(jnp.where(matches, owner_table[None, :], 0), axis=1)
     whole_keys, whole_values = (
         lax.all_gather(prefix_keys, "pre", axis=0, tiled=True),
         lax.all_gather(prefix_values, "pre", axis=0, tiled=True),
@@ -90,6 +98,275 @@
     return mixture.reshape(docs_here, span_len, features).astype(jnp.bfloat16)
 
 
+def attend(query, pieces, out):
+    for first in range(0, GROUPS, STACK):
+        heads = [slice((first + i) * HD, (first + i + 1) * HD) for i in range(STACK)]
+        rows = jnp.concatenate([query[:, head] for head in heads], axis=0)
+        scores, folded = [], None
+        for keys, _, visible in pieces:
+            score = lax.dot_general(rows, keys(), ROWS_BY_FEATURES, preferred_element_type=jnp.float32)
+            if visible is not None:
+                score = jnp.where(jnp.concatenate([visible] * STACK, axis=0), score, HIDDEN)
+            scores.append(score)
+            for at in range(0, score.shape[1], HD):
+                tile = score[:, at : at + HD]
+                folded = tile if folded is None else jnp.maximum(folded, tile)
+        peak = jnp.max(folded, axis=-1, keepdims=True) * LOG2_SCALE
+        folded, total = None, None
+        for (_, values, _), score in zip(pieces, scores):
+            weights = jnp.exp2(score * LOG2_SCALE - peak)
+            for at in range(0, score.shape[1], HD):
+                tile = weights[:, at : at + HD]
+                folded = tile if folded is None else folded + tile
+            added = lax.dot_general(
+                weights.astype(jnp.bfloat16), values(), ROWS_BY_KEYS, preferred_element_type=jnp.float32
+            )
+            total = added if total is None else total + added
+        result = (total / jnp.sum(folded, axis=-1, keepdims=True)).astype(jnp.bfloat16)
+        span = query.shape[0]
+        for i, head in enumerate(heads):
+            out[:, head] = result[i * span : (i + 1) * span]
+
+
+def masks(span, use_other):
+    row = lax.broadcasted_iota(jnp.int32, (span, span), 0)
+    column = lax.broadcasted_iota(jnp.int32, (span, span), 1)
+    return row >= column, row * 0 + use_other > 0
+
+
+def whole(ref):
+    return lambda: ref[...]
+
+
+def own_kernel(where, query, cache_keys, cache_values, keys, values, theirs, out):
+    span = keys.shape[1]
+    half = cache_keys.shape[1] // 2
+    causal, earlier = masks(span, where[0])
+    pieces = [
+        (whole(cache_keys.at[0, i * half : (i + 1) * half]), whole(cache_values.at[0, i * half : (i + 1) * half]), None)
+        for i in range(2)
+    ]
+    pieces.append((whole(keys.at[0]), whole(values.at[0]), causal))
+    pieces.append((whole(theirs.at[0, 0]), whole(theirs.at[0, 1]), earlier))
+    attend(query.at[0], pieces, out.at[0])
+
+
+def cache_pieces(caches, merged):
+    pieces = []
+    for piece in caches:
+        if merged:
+            one, other = piece
+            pieces.append(
+                (
+                    lambda one=one, other=other: one[0] + other[0],
+                    lambda one=one, other=other: one[1] + other[1],
+                    None,
+                )
+            )
+        else:
+            pieces.append((whole(piece.at[0]), whole(piece.at[1]), None))
+    return pieces
+
+
+def theirs_part(where, query, keys, values, theirs, pieces, out):
+    causal, earlier = masks(keys.shape[1], 1 - where[0])
+    pieces = pieces + [
+        (whole(theirs.at[0, 0]), whole(theirs.at[0, 1]), causal),
+        (whole(keys.at[0]), whole(values.at[0]), earlier),
+    ]
+    attend(query, pieces, out)
+
+
+def mine_part(where, query, keys, values, theirs, pieces, out):
+    causal, earlier = masks(keys.shape[1], where[0])
+    pieces = pieces + [
+        (whole(keys.at[0]), whole(values.at[0]), causal),
+        (whole(theirs.at[0, 0]), whole(theirs.at[0, 1]), earlier),
+    ]
+    attend(query, pieces, out)
+
+
+def both_kernel(counts, where, query, sent_query, keys, values, theirs, *rest):
+    pieces, rest = cache_pieces(rest[:counts], False), rest[counts:]
+    _, out, sent_out = rest
+
+    @pl.when(pl.program_id(0) == 0)
+    def _():
+        theirs_part(where, sent_query.at[0], keys, values, theirs, pieces, sent_out)
+
+    @pl.when(pl.program_id(0) == 1)
+    def _():
+        mine_part(where, query.at[0], keys, values, theirs, pieces, out.at[0])
+
+
+def theirs_kernel(where, sent_query, keys, values, theirs, *rest):
+    caches, (sent_out,) = rest[:-1], rest[-1:]
+    pieces = cache_pieces(list(zip(caches[0::2], caches[1::2])), True)
+    theirs_part(where, sent_query.at[0], keys, values, theirs, pieces, sent_out)
+
+
+def mine_kernel(where, query, keys, values, theirs, *rest):
+    caches, (_, out) = rest[:-2], rest[-2:]
+    pieces = cache_pieces(list(zip(caches[0::2], caches[1::2])), True)
+    mine_part(where, query.at[0], keys, values, theirs, pieces, out.at[0])
+
+
+def cost(rows, keys, moved):
+    return pl.CostEstimate(flops=4 * rows * keys * HD, transcendentals=rows * keys, bytes_accessed=moved)
+
+
+def exchanged(queries, doc_keys, doc_values, prefix_keys, prefix_values, holders):
+    me, stage = lax.axis_index("pre"), lax.axis_index("stg")
+    owners = lax.axis_size("pre")
+    docs, span, features = queries.shape
+    length = prefix_keys.shape[1]
+    half = length // 2
+    width = GROUPS * HD
+    other = 1 - stage
+
+    def over(axis, pairs):
+        return lambda block: lax.ppermute(block, axis, pairs)
+
+    near = over("pre", [(i, i ^ 1) for i in range(owners)])
+    far = over("pre", [(i, i ^ 2) for i in range(owners)])
+    middle = over("pre", [(1, 2), (2, 1)])
+    forward = over("pre", [(2, 3), (1, 0)])
+    partner = over("stg", [(0, 1), (1, 0)])
+
+    distance = holders ^ me
+    order = jnp.arange(docs, dtype=jnp.int32)
+    doc_at = [jnp.sum(jnp.where(distance == j, order, 0)) for j in range(owners)]
+    where = jnp.stack([stage] + doc_at).astype(jnp.int32)
+
+    cache = jnp.stack([prefix_keys[0], prefix_values[0]])
+    cache = lax.dynamic_slice_in_dim(cache, stage * HD, HD, 2)
+    first, second = cache[:, :half], cache[:, half:]
+    far_first, far_second = far(first), far(second)
+    near_first, near_second = near(first), near(second)
+
+    local = jnp.stack([doc_keys, doc_values], axis=1)
+    sent_local = jnp.concatenate(
+        [
+            lax.dynamic_slice_in_dim(local, other * HD, HD, 3),
+            lax.dynamic_slice(local, (doc_at[0], 0, 0, stage * HD), (1, 2, span, HD)),
+        ]
+    )
+    their_local = partner(sent_local)
+    sent_queries = jnp.concatenate(
+        [lax.dynamic_slice(queries, (doc_at[j], 0, other * width), (1, span, width)) for j in range(1, owners)]
+    )
+    their_queries = partner(sent_queries)
+
+    first, far_first = lax.optimization_barrier((first, far_first))
+    middle_first, forward_first = middle(first), forward(far_first)
+    second, far_second = lax.optimization_barrier((second, far_second))
+    middle_second, forward_second = middle(second), forward(far_second)
+
+    def call(kernel, in_specs, out_specs, out_shape, grid, name, work, aliases=None):
+        return pl.pallas_call(
+            kernel,
+            grid_spec=pltpu.PrefetchScalarGridSpec(
+                num_scalar_prefetch=1, grid=grid, in_specs=in_specs, out_specs=out_specs
+            ),
+            out_shape=out_shape,
+            input_output_aliases=aliases or {},
+            cost_estimate=work,
+            name=name,
+        )
+
+    def head(i, w):
+        return jnp.where(i == 0, w[0], 1 - w[0])
+
+    keys_all = length + 2 * span
+    step_bytes = 2 * 2 * (keys_all * HD + span * width)
+    answer = jax.ShapeDtypeStruct(queries.shape, jnp.bfloat16)
+    out = call(
+        own_kernel,
+        [
+            pl.BlockSpec((1, span, width), lambda i, w: (w[1], 0, head(i, w))),
+            pl.BlockSpec((1, length, HD), lambda i, w: (0, 0, head(i, w))),
+            pl.BlockSpec((1, length, HD), lambda i, w: (0, 0, head(i, w))),
+            pl.BlockSpec((1, span, HD), lambda i, w: (w[1], 0, head(i, w))),
+            pl.BlockSpec((1, span, HD), lambda i, w: (w[1], 0, head(i, w))),
+            pl.BlockSpec((1, 2, span, HD), lambda i, w: (jnp.where(i == 0, w[1], docs), 0, 0, 0)),
+        ],
+        pl.BlockSpec((1, span, width), lambda i, w: (w[1], 0, head(i, w))),
+        answer,
+        (2,),
+        "held",
+        cost(2 * GROUPS * span, keys_all, 2 * step_bytes),
+    )(where, queries, prefix_keys, prefix_values, doc_keys, doc_values, their_local)
+
+    sent = jax.ShapeDtypeStruct((span, width), jnp.bfloat16)
+
+    def specs(slot):
+        query = pl.BlockSpec((1, span, width), lambda i, w: (w[slot + 1], 0, w[0]))
+        their_query = pl.BlockSpec((1, span, width), lambda i, w: (slot - 1, 0, 0))
+        local = [
+            pl.BlockSpec((1, span, HD), lambda i, w: (w[slot + 1], 0, w[0])),
+            pl.BlockSpec((1, span, HD), lambda i, w: (w[slot + 1], 0, w[0])),
+            pl.BlockSpec((1, 2, span, HD), lambda i, w: (w[slot + 1], 0, 0, 0)),
+        ]
+        cached = pl.BlockSpec((2, half, HD), lambda i, w: (0, 0, 0))
+        mine = pl.BlockSpec((1, span, width), lambda i, w: (w[slot + 1], 0, w[0]))
+        theirs = pl.BlockSpec((span, width), lambda i, w: (0, 0))
+        return query, their_query, local, cached, mine, theirs
+
+    anywhere = pl.BlockSpec(memory_space=pl.ANY)
+    returned = []
+    for slot, caches in ((1, (near_first, near_second)), (2, (far_first, far_second))):
+        query, their_query, local_specs, cached, mine, theirs = specs(slot)
+        out, answer_sent = call(
+            functools.partial(both_kernel, 2),
+            [query, their_query, *local_specs, cached, cached, anywhere],
+            [mine, theirs],
+            [answer, sent],
+            (2,),
+            f"slot{slot}",
+            cost(2 * GROUPS * span, keys_all, 2 * step_bytes),
+            {8: 0},
+        )(where, queries, their_queries, doc_keys, doc_values, their_local, *caches, out)
+        returned.append(partner(answer_sent))
+
+    slot = owners - 1
+    caches = (middle_first, forward_first, middle_second, forward_second)
+    query, their_query, local_specs, cached, mine, theirs = specs(slot)
+    answer_sent = call(
+        theirs_kernel,
+        [their_query, *local_specs, *[cached] * 4],
+        theirs,
+        sent,
+        (1,),
+        "last_theirs",
+        cost(GROUPS * span, keys_all, step_bytes),
+    )(where, their_queries, doc_keys, doc_values, their_local, *caches)
+    returned.append(partner(answer_sent))
+    out = call(
+        mine_kernel,
+        [query, *local_specs, *[cached] * 4, anywhere],
+        mine,
+        answer,
+        (1,),
+        "last_mine",
+        cost(GROUPS * span, keys_all, step_bytes),
+        {9: 0},
+    )(where, queries, doc_keys, doc_values, their_local, *caches, out)
+    for slot, block in enumerate(returned, 1):
+        out = lax.dynamic_update_slice(out, block[None], (doc_at[slot], 0, other * width))
+    return out
+
+
+def shards(queries, doc_keys, doc_values, prefix_keys, prefix_values, template, owner_table):
+    templates_all = owner_table.shape[0]
+    matches = template == jnp.arange(templates_all, dtype=jnp.int32)[None, :]
+    holders = jnp.sum(jnp.where(matches, owner_table[None, :], 0), axis=1)
+    owners, stages, heads = lax.axis_size("pre"), lax.axis_size("stg"), KVH // lax.axis_size("tp")
+    docs, span, _ = queries.shape
+    paired = owners == docs == templates_all == 4 and stages == heads == 2
+    program = exchanged if paired and span == HD and prefix_keys.shape[1] % (2 * HD) == 0 else gathered
+    return program(queries, doc_keys, doc_values, prefix_keys, prefix_values, holders)
+
+
 def solution(mesh):
     return jax.shard_map(
         shards,

time: 163 us -> 91.1 us (0.56)
  the two profiles are of different devices: /device:TPU:0 before, /device:TPU:16 now
where the time goes in v1:
time: 91.1 us; the launch traced here: 90.6 us
  Pallas kernels  35.7 us (39%)
  starting transfers between devices  24.5 us (27%)
  waiting for transfers between devices  11.2 us (12%)
  local copies, waits for them, and re-layouts  9.56 us (10%)
  between operations  7.68 us (8%)
  other arithmetic  1.91 us (2%)
    ppermute x13, starting transfers between devices, over(): return lambda block: lax.ppermute(block, axis, pairs)  24.5 us
    pallas_call x2, Pallas kernels, exchanged(): call(functools.partial(both_kernel, 2), [query, their_query, *local_specs...  16.6 us
    ppermute x13, waiting for transfers between devices, over(): return lambda block: lax.ppermute(block, axis, pairs)  11.2 us
    pallas_call x1, Pallas kernels, exchanged(): call(own_kernel, [pl.BlockSpec((1, span, width), lambda i, w: (w[1], 0, h...  8.11 us
    pallas_call x1, Pallas kernels, exchanged(): call(theirs_kernel, [their_query, *local_specs, *[cached] * 4], theirs, s...  5.53 us
    pallas_call x1, Pallas kernels, exchanged(): call(mine_kernel, [query, *local_specs, *[cached] * 4, anywhere], mine, a...  5.51 us
    another operation x1, local copies, waits for them, and re-layouts, exchanged(): where = jnp.stack([stage] + doc_at).astype(jnp.int32)  3.05 us
    unnamed x24, local copies, waits for them, and re-layouts  2.42 us
  transfers between devices with their start and end apart: 13, of which 1 were waited for; matrix products, arithmetic and copies ran while one was open for 6% of the time, Pallas kernels for 39%

profile of v1, /device:TPU:16, one launch (start us, length us, event | category | flops | bytes accessed | tf_op | source)
XLA Modules:
  0.0 90.6 jit_solution(12063123200562481429)
XLA Ops:
  0.0 0.9 %select_reduce_fusion = s32[4]{0:T(128)S(1)} fusion(s32[4]{0:T(128)} %param.13, s32[4]{0:T(128)} %bitcast.18), kind=kLoop, calls=%fused_computation.17 | loop fusion | flops 44 | bytes 48 | tf_op jit(solution)/shard_map/reduce_sum | solution.py:362
  0.9 0.7 fusion.6
  7.3 1.2 %constant_dynamic-slice_fusion.2 = (bf16[1,128,1024]{2,1,0:T(8,128)(2,1)S(1)}, bf16[1,128,1024]{2,1,0:T(8,128)(2,1)S(1)}, bf16[1,128,1024]{2,1,0:T(8,128)(2,1)S(1)}) fusion(bf16[4,128,2048]{2,1,0:T(8,128)(2,1)} %query.7, s32[]{:T(128)S(6)} %select_n.55, s32[]{:T(128)S(6)} %select_n.56, s32[]{:T(128)S(6)} %select_n.58, s32[]{:T(128)S(6)} %select_n.57), kind=kLoop, calls=%fused_computation.16 | loop fusion | bytes 1572880 | tf_op jit(solution)/shard_map/dynamic_slice | solution.py:256
  8.4 0.0 copy-start
  8.4 0.0 copy-start.1
  8.5 0.1 pad_maximum_fusion
  8.6 1.6 %collective-permute-start.7 = (bf16[3,128,1024]{2,1,0:T(8,128)(2,1)S(1)}, bf16[3,128,1024]{2,1,0:T(8,128)(2,1)S(1)}, u32[]{:S(2)}, u32[]{:S(2)}) collective-permute-start(bf16[3,128,1024]{2,1,0:T(8,128)(2,1)S(1)} %pad_maximum_fusion), channel_id=1, source_target_pairs={{0,2},{2,0},{1,3},{3,1},{4,6},{6,4},{5,7},{7,5},{8,10},{10,8},{9,1... | collective-permute-start | bytes 2359304 | tf_op jit(solution)/shard_map/ppermute | solution.py:228
  10.1 0.0 copy-done.5
  10.2 0.8 fusion.7
  10.9 0.3 collective-permute-start.4
  13.2 0.1 fusion.1
  13.3 0.3 collective-permute-start
  13.6 2.9 %collective-permute-start.1 = (bf16[2,512,128]{2,1,0:T(8,128)(2,1)S(1)}, bf16[2,512,128]{2,1,0:T(8,128)(2,1)S(1)}, u32[]{:S(2)}, u32[]{:S(2)}) collective-permute-start(bf16[2,512,128]{2,1,0:T(8,128)(2,1)S(1)} %get-tuple-element.13), channel_id=1, source_target_pairs={{0,8},{4,12},{8,0},{12,4},{1,9},{5,13},{9,1},{13,5},{2,10},{6,14},... | collective-permute-start | bytes 786440 | tf_op jit(solution)/shard_map/ppermute | solution.py:228
  16.5 1.6 %collective-permute-start.8 = (bf16[2,512,128]{2,1,0:T(8,128)(2,1)S(1)}, bf16[2,512,128]{2,1,0:T(8,128)(2,1)}, u32[]{:S(2)}, u32[]{:S(2)}) collective-permute-start(bf16[2,512,128]{2,1,0:T(8,128)(2,1)S(1)} %get-tuple-element.13), channel_id=1, source_target_pairs={{0,4},{4,0},{8,12},{12,8},{1,5},{5,1},{9,13},{13,9},{2,6},{6,2},{1... | collective-permute-start | bytes 786440 | tf_op jit(solution)/shard_map/ppermute | solution.py:228
  18.1 11.1 %collective-permute-done.4.rest_1_ = bf16[2,512,128]{2,1,0:T(8,128)(2,1)S(1)} collective-permute-done((bf16[2,512,128]{2,1,0:T(8,128)(2,1)}, bf16[2,512,128]{2,1,0:T(8,128)(2,1)S(1)}, u32[]{:S(2)}, u32[]{:S(2)}) %collective-permute-start.4) | collective-permute-done | bytes 262176 | tf_op jit(solution)/shard_map/ppermute | solution.py:228
  29.2 3.4 %collective-permute-start.9 = (bf16[2,512,128]{2,1,0:T(8,128)(2,1)}, bf16[2,512,128]{2,1,0:T(8,128)(2,1)}, u32[]{:S(2)}, u32[]{:S(2)}) collective-permute-start(bf16[2,512,128]{2,1,0:T(8,128)(2,1)} %get-tuple-element.15), channel_id=1, source_target_pairs={{0,4},{4,0},{8,12},{12,8},{1,5},{5,1},{9,13},{13,9},{2,6},{6,2},{1... | collective-permute-start | bytes 786440 | tf_op jit(solution)/shard_map/ppermute | solution.py:228
  32.6 3.0 %stack.35.where = s32[5]{0:T(128)} concatenate(s32[1]{0:T(128)} %bitcast, s32[1]{0:T(128)} %bitcast.2, s32[1]{0:T(128)} %bitcast.3, s32[1]{0:T(128)} %bitcast.4, s32[1]{0:T(128)} %bitcast.5), dimensions={0} | concatenate | bytes 40 | tf_op jit(solution)/shard_map/stack | solution.py:239
  35.6 0.0 collective-permute-done.1.rest_0_
  35.6 4.5 %collective-permute-start.6 = (bf16[2,512,128]{2,1,0:T(8,128)(2,1)S(1)}, bf16[2,512,128]{2,1,0:T(8,128)(2,1)S(1)}, u32[]{:S(2)}, u32[]{:S(2)}) collective-permute-start(bf16[2,512,128]{2,1,0:T(8,128)(2,1)S(1)} %collective-permute-done.4.rest_1_), channel_id=1, source_target_pairs={{8,12},{4,0},{9,13},{5,1},{10,14},{6,2},{11,15},{7,3},{24,28},{20,... | collective-permute-start | bytes 786440 | tf_op jit(solution)/shard_map/ppermute | solution.py:228
  40.1 0.0 collective-permute-done.theirs
  40.1 1.3 %collective-permute-start.3 = (bf16[2,512,128]{2,1,0:T(8,128)(2,1)S(1)}, bf16[2,512,128]{2,1,0:T(8,128)(2,1)S(1)}, u32[]{:S(2)}, u32[]{:S(2)}) collective-permute-start(bf16[2,512,128]{2,1,0:T(8,128)(2,1)S(1)} %collective-permute-done.1.rest_0_), channel_id=1, source_target_pairs={{8,12},{4,0},{9,13},{5,1},{10,14},{6,2},{11,15},{7,3},{24,28},{20,... | collective-permute-start | bytes 786440 | tf_op jit(solution)/shard_map/ppermute | solution.py:228
  41.5 8.1 %held.1.rest_2_ = bf16[4,128,2048]{2,1,0:T(8,128)(2,1)} custom-call(s32[5]{0:T(128)} %stack.35.where, bf16[4,128,2048]{2,1,0:T(8,128)(2,1)} %query.7, bf16[1,1024,256]{2,1,0:T(8,128)(2,1)} %cache_keys.1, bf16[1,1024,256]{2,1,0:T(8,128)(2,1)} %cache_values.1, bf16[4,128,256]{2,1,0:T(8,128)(2,1)} %keys.9, bf16[4,128,256]{2,1,0:T(8,128)(2,1)} %values.9, ...), custom_call_target="tpu_custom_call" | custom-call | flops 1342177280 | bytes 2359296 | tf_op jit(solution)/shard_map/held/pallas_call | solution.py:283
  49.6 0.0 collective-permute-done.8.rest_0_
  49.6 1.9 %collective-permute-start.5 = (bf16[2,512,128]{2,1,0:T(8,128)(2,1)}, bf16[2,512,128]{2,1,0:T(8,128)(2,1)S(1)}, u32[]{:S(2)}, u32[]{:S(2)}) collective-permute-start(bf16[2,512,128]{2,1,0:T(8,128)(2,1)} %get-tuple-element.15), channel_id=1, source_target_pairs={{4,8},{8,4},{5,9},{9,5},{6,10},{10,6},{7,11},{11,7},{20,24},{24,20... | collective-permute-start | bytes 786440 | tf_op jit(solution)/shard_map/ppermute | solution.py:228
  51.5 0.0 collective-permute-done.9.rest_1_
  51.5 4.1 %collective-permute-start.2 = (bf16[2,512,128]{2,1,0:T(8,128)(2,1)S(1)}, bf16[2,512,128]{2,1,0:T(8,128)(2,1)S(1)}, u32[]{:S(2)}, u32[]{:S(2)}) collective-permute-start(bf16[2,512,128]{2,1,0:T(8,128)(2,1)S(1)} %get-tuple-element.13), channel_id=1, source_target_pairs={{4,8},{8,4},{5,9},{9,5},{6,10},{10,6},{7,11},{11,7},{20,24},{24,20... | collective-permute-start | bytes 786440 | tf_op jit(solution)/shard_map/ppermute | solution.py:228
  55.6 0.0 collective-permute-done.7.sent_query
  55.6 0.9 copy-done.3
  56.5 8.3 %slot1.1 = (bf16[4,128,2048]{2,1,0:T(8,128)(2,1)}, bf16[128,1024]{1,0:T(8,128)(2,1)}) custom-call(s32[5]{0:T(128)} %stack.35.where, bf16[4,128,2048]{2,1,0:T(8,128)(2,1)} %query.7, bf16[3,128,1024]{2,1,0:T(8,128)(2,1)} %copy-done.3, bf16[4,128,256]{2,1,0:T(8,128)(2,1)} %keys.9, bf16[4,128,256]{2,1,0:T(8,128)(2,1)} %values.9, ...), custom_call_target="tpu_custom_call", output_to_operand_aliasing={{0}: (8, {})} | custom-call | flops 1342177280 | bytes 2359296 | tf_op jit(solution)/shard_map/slot1/pallas_call | solution.py:319
  64.8 0.6 collective-permute-start.10
  65.4 8.3 %slot2.1 = (bf16[4,128,2048]{2,1,0:T(8,128)(2,1)}, bf16[128,1024]{1,0:T(8,128)(2,1)}) custom-call(s32[5]{0:T(128)} %stack.35.where, bf16[4,128,2048]{2,1,0:T(8,128)(2,1)} %query.7, bf16[3,128,1024]{2,1,0:T(8,128)(2,1)} %copy-done.3, bf16[4,128,256]{2,1,0:T(8,128)(2,1)} %keys.9, bf16[4,128,256]{2,1,0:T(8,128)(2,1)} %values.9, ...), custom_call_target="tpu_custom_call", output_to_operand_aliasing={{0}: (8, {})} | custom-call | flops 1342177280 | bytes 2359296 | tf_op jit(solution)/shard_map/slot2/pallas_call | solution.py:319
  73.7 0.0 collective-permute-done.6.rest_3_
  73.7 1.5 %collective-permute-start.11 = (bf16[128,1024]{1,0:T(8,128)(2,1)}, bf16[128,1024]{1,0:T(8,128)(2,1)S(1)}, u32[]{:S(2)}, u32[]{:S(2)}) collective-permute-start(bf16[128,1024]{1,0:T(8,128)(2,1)} %get-tuple-element.20), channel_id=1, source_target_pairs={{0,2},{2,0},{1,3},{3,1},{4,6},{6,4},{5,7},{7,5},{8,10},{10,8},{9,1... | collective-permute-start | bytes 786440 | tf_op jit(solution)/shard_map/ppermute | solution.py:228
  75.2 0.0 collective-permute-done.3.rest_1_
  75.2 0.0 collective-permute-done.5.rest_2_
  75.2 0.0 collective-permute-done.2.rest_0_
  75.3 0.7 copy-done.7
  75.9 0.1 copy-done.8
  76.0 0.7 copy-done.9
  76.7 5.5 %last_theirs.1 = bf16[128,1024]{1,0:T(8,128)(2,1)} custom-call(s32[5]{0:T(128)} %stack.35.where, bf16[3,128,1024]{2,1,0:T(8,128)(2,1)} %copy-done.3, bf16[4,128,256]{2,1,0:T(8,128)(2,1)} %keys.9, bf16[4,128,256]{2,1,0:T(8,128)(2,1)} %values.9, bf16[5,2,128,128]{3,2,1,0:T(8,128)(2,1)} %copy-done.2, bf16[2,512,128]{2,1,0:T(8,128)(2,1)} %copy-done.9, ...), custom_call_target="tpu_custom_call" | custom-call | flops 671088640 | bytes 1179648 | tf_op jit(solution)/shard_map/last_theirs/pallas_call | solution.py:334
  82.3 0.6 collective-permute-start.12
  82.9 5.5 %last_mine.1 = bf16[4,128,2048]{2,1,0:T(8,128)(2,1)} custom-call(s32[5]{0:T(128)} %stack.35.where, bf16[4,128,2048]{2,1,0:T(8,128)(2,1)} %query.7, bf16[4,128,256]{2,1,0:T(8,128)(2,1)} %keys.9, bf16[4,128,256]{2,1,0:T(8,128)(2,1)} %values.9, bf16[5,2,128,128]{3,2,1,0:T(8,128)(2,1)} %copy-done.2, ...), custom_call_target="tpu_custom_call", output_to_operand_aliasing={{}: (9, {})} | custom-call | flops 671088640 | bytes 1179648 | tf_op jit(solution)/shard_map/last_mine/pallas_call | solution.py:344
  88.4 0.0 collective-permute-done.10
  88.4 0.7 bitcast_dynamic-update-slice_fusion.2
  89.1 0.0 collective-permute-done.11
  89.1 0.7 bitcast_dynamic-update-slice_fusion.1
  89.8 0.0 collective-permute-done.12
  89.8 0.7 bitcast_dynamic-update-slice_fusion
  (20 shorter events, 0.1 us)
Async XLA Ops:
  0.0 10.1 %copy-start.4 = (bf16[1,1024,256]{2,1,0:T(8,128)(2,1)S(1)}, bf16[1,1024,256]{2,1,0:T(8,128)(2,1)}, u32[]{:S(2)}) copy-start(bf16[1,1024,256]{2,1,0:T(8,128)(2,1)} %cache_keys.1) | copy-start | bytes 1572868
  0.0 10.1 %copy-start.5 = (bf16[1,1024,256]{2,1,0:T(8,128)(2,1)S(1)}, bf16[1,1024,256]{2,1,0:T(8,128)(2,1)}, u32[]{:S(2)}) copy-start(bf16[1,1024,256]{2,1,0:T(8,128)(2,1)} %cache_values.1) | copy-start | bytes 1572868
  8.4 4.7 %copy-start = (bf16[4,128,256]{2,1,0:T(8,128)(2,1)S(1)}, bf16[4,128,256]{2,1,0:T(8,128)(2,1)}, u32[]{:S(2)}) copy-start(bf16[4,128,256]{2,1,0:T(8,128)(2,1)} %keys.9) | copy-start | bytes 786436
  8.4 4.7 %copy-start.1 = (bf16[4,128,256]{2,1,0:T(8,128)(2,1)S(1)}, bf16[4,128,256]{2,1,0:T(8,128)(2,1)}, u32[]{:S(2)}) copy-start(bf16[4,128,256]{2,1,0:T(8,128)(2,1)} %values.9) | copy-start | bytes 786436
  8.6 47.1 %collective-permute-start.7 = (bf16[3,128,1024]{2,1,0:T(8,128)(2,1)S(1)}, bf16[3,128,1024]{2,1,0:T(8,128)(2,1)S(1)}, u32[]{:S(2)}, u32[]{:S(2)}) collective-permute-start(bf16[3,128,1024]{2,1,0:T(8,128)(2,1)S(1)} %pad_maximum_fusion), channel_id=1, source_target_pairs={{0,2},{2,0},{1,3},{3,1},{4,6},{6,4},{5,7},{7,5},{8,10},{10,8},{9,1... | collective-permute-start | bytes 2359304 | tf_op jit(solution)/shard_map/ppermute | solution.py:228
  10.9 18.3 %collective-permute-start.4 = (bf16[2,512,128]{2,1,0:T(8,128)(2,1)}, bf16[2,512,128]{2,1,0:T(8,128)(2,1)S(1)}, u32[]{:S(2)}, u32[]{:S(2)}) collective-permute-start(bf16[2,512,128]{2,1,0:T(8,128)(2,1)} %get-tuple-element.15), channel_id=1, source_target_pairs={{0,8},{4,12},{8,0},{12,4},{1,9},{5,13},{9,1},{13,5},{2,10},{6,14},... | collective-permute-start | bytes 786440 | tf_op jit(solution)/shard_map/ppermute | solution.py:228
  13.3 26.8 %collective-permute-start = (bf16[5,2,128,128]{3,2,1,0:T(8,128)(2,1)S(1)}, bf16[5,2,128,128]{3,2,1,0:T(8,128)(2,1)S(1)}, u32[]{:S(2)}, u32[]{:S(2)}) collective-permute-start(bf16[5,2,128,128]{3,2,1,0:T(8,128)(2,1)S(1)} %pad_maximum_fusion.1), channel_id=1, source_target_pairs={{0,2},{2,0},{1,3},{3,1},{4,6},{6,4},{5,7},{7,5},{8,10},{10,8},{9,1... | collective-permute-start | bytes 983048 | tf_op jit(solution)/shard_map/ppermute | solution.py:228
  13.6 22.1 %collective-permute-start.1 = (bf16[2,512,128]{2,1,0:T(8,128)(2,1)S(1)}, bf16[2,512,128]{2,1,0:T(8,128)(2,1)S(1)}, u32[]{:S(2)}, u32[]{:S(2)}) collective-permute-start(bf16[2,512,128]{2,1,0:T(8,128)(2,1)S(1)} %get-tuple-element.13), channel_id=1, source_target_pairs={{0,8},{4,12},{8,0},{12,4},{1,9},{5,13},{9,1},{13,5},{2,10},{6,14},... | collective-permute-start | bytes 786440 | tf_op jit(solution)/shard_map/ppermute | solution.py:228
  16.5 33.1 %collective-permute-start.8 = (bf16[2,512,128]{2,1,0:T(8,128)(2,1)S(1)}, bf16[2,512,128]{2,1,0:T(8,128)(2,1)}, u32[]{:S(2)}, u32[]{:S(2)}) collective-permute-start(bf16[2,512,128]{2,1,0:T(8,128)(2,1)S(1)} %get-tuple-element.13), channel_id=1, source_target_pairs={{0,4},{4,0},{8,12},{12,8},{1,5},{5,1},{9,13},{13,9},{2,6},{6,2},{1... | collective-permute-start | bytes 786440 | tf_op jit(solution)/shard_map/ppermute | solution.py:228
  29.2 36.2 %copy-start.10 = (bf16[2,512,128]{2,1,0:T(8,128)(2,1)}, bf16[2,512,128]{2,1,0:T(8,128)(2,1)S(1)}, u32[]{:S(2)}) copy-start(bf16[2,512,128]{2,1,0:T(8,128)(2,1)S(1)} %collective-permute-done.4.rest_1_) | copy-start | bytes 786436
  29.2 22.3 %collective-permute-start.9 = (bf16[2,512,128]{2,1,0:T(8,128)(2,1)}, bf16[2,512,128]{2,1,0:T(8,128)(2,1)}, u32[]{:S(2)}, u32[]{:S(2)}) collective-permute-start(bf16[2,512,128]{2,1,0:T(8,128)(2,1)} %get-tuple-element.15), channel_id=1, source_target_pairs={{0,4},{4,0},{8,12},{12,8},{1,5},{5,1},{9,13},{13,9},{2,6},{6,2},{1... | collective-permute-start | bytes 786440 | tf_op jit(solution)/shard_map/ppermute | solution.py:228
  35.6 29.8 %copy-start.11 = (bf16[2,512,128]{2,1,0:T(8,128)(2,1)}, bf16[2,512,128]{2,1,0:T(8,128)(2,1)S(1)}, u32[]{:S(2)}) copy-start(bf16[2,512,128]{2,1,0:T(8,128)(2,1)S(1)} %collective-permute-done.1.rest_0_) | copy-start | bytes 786436
  35.6 38.1 %collective-permute-start.6 = (bf16[2,512,128]{2,1,0:T(8,128)(2,1)S(1)}, bf16[2,512,128]{2,1,0:T(8,128)(2,1)S(1)}, u32[]{:S(2)}, u32[]{:S(2)}) collective-permute-start(bf16[2,512,128]{2,1,0:T(8,128)(2,1)S(1)} %collective-permute-done.4.rest_1_), channel_id=1, source_target_pairs={{8,12},{4,0},{9,13},{5,1},{10,14},{6,2},{11,15},{7,3},{24,28},{20,... | collective-permute-start | bytes 786440 | tf_op jit(solution)/shard_map/ppermute | solution.py:228
  40.1 1.3 %copy-start.2 = (bf16[5,2,128,128]{3,2,1,0:T(8,128)(2,1)}, bf16[5,2,128,128]{3,2,1,0:T(8,128)(2,1)S(1)}, u32[]{:S(2)}) copy-start(bf16[5,2,128,128]{3,2,1,0:T(8,128)(2,1)S(1)} %collective-permute-done.theirs) | copy-start | bytes 983044
  40.1 35.1 %collective-permute-start.3 = (bf16[2,512,128]{2,1,0:T(8,128)(2,1)S(1)}, bf16[2,512,128]{2,1,0:T(8,128)(2,1)S(1)}, u32[]{:S(2)}, u32[]{:S(2)}) collective-permute-start(bf16[2,512,128]{2,1,0:T(8,128)(2,1)S(1)} %collective-permute-done.1.rest_0_), channel_id=1, source_target_pairs={{8,12},{4,0},{9,13},{5,1},{10,14},{6,2},{11,15},{7,3},{24,28},{20,... | collective-permute-start | bytes 786440 | tf_op jit(solution)/shard_map/ppermute | solution.py:228
  49.6 25.7 %collective-permute-start.5 = (bf16[2,512,128]{2,1,0:T(8,128)(2,1)}, bf16[2,512,128]{2,1,0:T(8,128)(2,1)S(1)}, u32[]{:S(2)}, u32[]{:S(2)}) collective-permute-start(bf16[2,512,128]{2,1,0:T(8,128)(2,1)} %get-tuple-element.15), channel_id=1, source_target_pairs={{4,8},{8,4},{5,9},{9,5},{6,10},{10,6},{7,11},{11,7},{20,24},{24,20... | collective-permute-start | bytes 786440 | tf_op jit(solution)/shard_map/ppermute | solution.py:228
  51.5 23.7 %collective-permute-start.2 = (bf16[2,512,128]{2,1,0:T(8,128)(2,1)S(1)}, bf16[2,512,128]{2,1,0:T(8,128)(2,1)S(1)}, u32[]{:S(2)}, u32[]{:S(2)}) collective-permute-start(bf16[2,512,128]{2,1,0:T(8,128)(2,1)S(1)} %get-tuple-element.13), channel_id=1, source_target_pairs={{4,8},{8,4},{5,9},{9,5},{6,10},{10,6},{7,11},{11,7},{20,24},{24,20... | collective-permute-start | bytes 786440 | tf_op jit(solution)/shard_map/ppermute | solution.py:228
  55.6 0.9 %copy-start.3 = (bf16[3,128,1024]{2,1,0:T(8,128)(2,1)}, bf16[3,128,1024]{2,1,0:T(8,128)(2,1)S(1)}, u32[]{:S(2)}) copy-start(bf16[3,128,1024]{2,1,0:T(8,128)(2,1)S(1)} %collective-permute-done.7.sent_query) | copy-start | bytes 2359300
  64.8 23.6 %collective-permute-start.10 = (bf16[128,1024]{1,0:T(8,128)(2,1)}, bf16[128,1024]{1,0:T(8,128)(2,1)S(1)}, u32[]{:S(2)}, u32[]{:S(2)}) collective-permute-start(bf16[128,1024]{1,0:T(8,128)(2,1)} %get-tuple-element.19), channel_id=1, source_target_pairs={{0,2},{2,0},{1,3},{3,1},{4,6},{6,4},{5,7},{7,5},{8,10},{10,8},{9,1... | collective-permute-start | bytes 786440 | tf_op jit(solution)/shard_map/ppermute | solution.py:228
  73.7 1.5 %copy-start.6 = (bf16[2,512,128]{2,1,0:T(8,128)(2,1)}, bf16[2,512,128]{2,1,0:T(8,128)(2,1)S(1)}, u32[]{:S(2)}) copy-start(bf16[2,512,128]{2,1,0:T(8,128)(2,1)S(1)} %collective-permute-done.6.rest_3_) | copy-start | bytes 786436
  73.7 15.4 %collective-permute-start.11 = (bf16[128,1024]{1,0:T(8,128)(2,1)}, bf16[128,1024]{1,0:T(8,128)(2,1)S(1)}, u32[]{:S(2)}, u32[]{:S(2)}) collective-permute-start(bf16[128,1024]{1,0:T(8,128)(2,1)} %get-tuple-element.20), channel_id=1, source_target_pairs={{0,2},{2,0},{1,3},{3,1},{4,6},{6,4},{5,7},{7,5},{8,10},{10,8},{9,1... | collective-permute-start | bytes 786440 | tf_op jit(solution)/shard_map/ppermute | solution.py:228
  75.2 0.7 copy-start.7
  75.2 0.8 copy-start.8
  76.0 0.7 copy-start.9
  82.3 7.6 %collective-permute-start.12 = (bf16[128,1024]{1,0:T(8,128)(2,1)}, bf16[128,1024]{1,0:T(8,128)(2,1)S(1)}, u32[]{:S(2)}, u32[]{:S(2)}) collective-permute-start(bf16[128,1024]{1,0:T(8,128)(2,1)} %last_theirs.1), channel_id=1, source_target_pairs={{0,2},{2,0},{1,3},{3,1},{4,6},{6,4},{5,7},{7,5},{8,10},{10,8},{9,1... | collective-permute-start | bytes 786440 | tf_op jit(solution)/shard_map/ppermute | solution.py:228

commit v2 on v0

--- a/solution.py
+++ b/solution.py
@@ -1,11 +1,22 @@
+import functools
+import math
+
 import jax
 import jax.numpy as jnp
 from jax import lax
+from jax.experimental import pallas as pl
+from jax.experimental.pallas import tpu as pltpu
 from jax.sharding import PartitionSpec as P
 
 H = 32
 KVH = 4
 HD = 128
+GROUPS = H // KVH
+STACK = 2
+LOG2_SCALE = HD**-0.5 * math.log2(math.e)
+HIDDEN = -1e30
+ROWS_BY_FEATURES = (((1,), (1,)), ((), ()))
+ROWS_BY_KEYS = (((1,), (0,)), ((), ()))
 
 
 def prefix_part(rows_in, cache_keys, cache_values, kv_local):
@@ -35,13 +46,10 @@
     )
 
 
-def shards(queries, doc_keys, doc_values, prefix_keys, prefix_values, template, owner_table):
+def gathered(queries, doc_keys, doc_values, prefix_keys, prefix_values, holders):
     kv_local = KVH // lax.axis_size("tp")
     groups = H // KVH
     docs_here, span_len, features = queries.shape
-    templates_all = owner_table.shape[0]
-    matches = template == jnp.arange(templates_all, dtype=jnp.int32)[None, :]
-    holders = jnp.sum(jnp.where(matches, owner_table[None, :], 0), axis=1)
     whole_keys, whole_values = (
         lax.all_gather(prefix_keys, "pre", axis=0, tiled=True),
         lax.all_gather(prefix_values, "pre", axis=0, tiled=True),
@@ -90,6 +98,309 @@
     return mixture.reshape(docs_here, span_len, features).astype(jnp.bfloat16)
 
 
+def head_slice(column):
+    return pl.ds(pl.multiple_of(column, HD), HD)
+
+
+def attend_kernel(plan, length, where, queries, *refs):
+    stage, doc = where[0], where[plan["slot"] + 1]
+    other = 1 - stage
+    their_queries, refs = (refs[0], refs[1:]) if plan["their_queries"] else (None, refs)
+    doc_keys, doc_values, their_local, *caches = refs[: 3 + plan["caches"]]
+    refs = refs[3 + plan["caches"] + plan["aliased"] :]
+    outs, (rows, keys, values, scores, results, sems) = refs[: plan["outs"]], refs[plan["outs"] :]
+    span = doc_keys.shape[1]
+    block = scores.shape[1]
+    stack = block // span
+    parts = plan["parts"]
+    used = [0]
+
+    def begin(source, target, ready=None, instead=None):
+        sem = sems.at[used[0]]
+        used[0] += 1
+        copy = pltpu.make_async_copy(source, target, sem)
+        if ready is None:
+            copy.start()
+        else:
+            pl.when(ready)(copy.start)
+            pl.when(jnp.logical_not(ready))(pltpu.make_async_copy(instead, target, sem).start)
+        return copy
+
+    def fetch_rows(at, mine, head):
+        source = queries.at[doc] if mine else their_queries.at[plan["sent_at"]]
+        base = head * (GROUPS * HD) if mine else 0
+        return [
+            begin(source.at[:, head_slice(base + g * HD)], rows.at[at, g * span : (g + 1) * span]) for g in range(GROUPS)
+        ]
+
+    def fetch_side(side, at, head):
+        target, local = ((keys, doc_keys), (values, doc_values))[side]
+        cut = slice(0, HD)
+        copies = []
+        if plan["slot"] == 0:
+            copies.append(begin(caches[side].at[0, :, head_slice(head * HD)], target.at[at, :length, cut]))
+            theirs = doc if at == 0 else plan["extra"]
+        elif plan["slot"] == 3:
+            half = length // 2
+            for i in range(2):
+                copies.append(
+                    begin(
+                        caches[i].at[side],
+                        target.at[at, i * half : (i + 1) * half, cut],
+                        where[5] > 0,
+                        caches[2].at[side, i * half : (i + 1) * half],
+                    )
+                )
+            theirs = doc
+        else:
+            size = length // len(caches)
+            for i, cache in enumerate(caches):
+                copies.append(begin(cache.at[side], target.at[at, i * size : (i + 1) * size, cut]))
+            theirs = doc
+        copies.append(begin(local.at[doc, :, head_slice(head * HD)], target.at[at, length : length + span, cut]))
+        copies.append(begin(their_local.at[theirs, side], target.at[at, length + span :, cut]))
+        return copies
+
+    row_copies, key_copies, value_copies = {}, {}, {}
+    for at, (mine, own_head) in enumerate(parts):
+        head = stage if own_head else other
+        row_copies[at] = fetch_rows(at, mine, head)
+        if at < keys.shape[0]:
+            key_copies[at] = fetch_side(0, at, head)
+            value_copies[at] = fetch_side(1, at, head)
+    values[:, :, HD:] = jnp.ones(values.shape[:2] + (HD,), values.dtype)
+
+    line = lax.broadcasted_iota(jnp.int32, (block, span), 0) % span
+    column = lax.broadcasted_iota(jnp.int32, (block, span), 1)
+    causal = line >= column
+
+    def score(number):
+        at, first = divmod(number, GROUPS // stack)
+        mine = parts[at][0]
+        held = min(at, keys.shape[0] - 1)
+        for copies in (row_copies, key_copies):
+            for copy in copies.pop(at, ()):
+                copy.wait()
+        query = rows[at, first * block : (first + 1) * block]
+        made = lax.dot_general(query, keys[held], ROWS_BY_FEATURES, preferred_element_type=jnp.float32)
+        earlier = line * 0 + (stage if mine else other) > 0
+        own, theirs = (causal, earlier) if mine else (earlier, causal)
+        slot = number % 2
+        scores[slot, :, :length] = made[:, :length]
+        scores[slot, :, length : length + span] = jnp.where(own, made[:, length : length + span], HIDDEN)
+        scores[slot, :, length + span :] = jnp.where(theirs, made[:, length + span :], HIDDEN)
+
+    def weigh(number):
+        at, first = divmod(number, GROUPS // stack)
+        held = min(at, keys.shape[0] - 1)
+        for copy in value_copies.pop(at, ()):
+            copy.wait()
+        made = scores[number % 2]
+        peak = made[:, :HD]
+        for start in range(HD, made.shape[1], HD):
+            peak = jnp.maximum(peak, made[:, start : start + HD])
+        peak = jnp.max(peak, axis=-1, keepdims=True) * LOG2_SCALE
+        weights = jnp.exp2(made * LOG2_SCALE - peak).astype(jnp.bfloat16)
+        added = lax.dot_general(weights, values[held], ROWS_BY_KEYS, preferred_element_type=jnp.float32)
+        result = (added[:, :HD] / added[:, HD:]).astype(jnp.bfloat16)
+        for i in range(stack):
+            group = first * stack + i
+            results[at, :, group * HD : (group + 1) * HD] = result[i * span : (i + 1) * span]
+
+    blocks = len(parts) * GROUPS // stack
+    finished = []
+    score(0)
+    for number in range(blocks):
+        if number + 1 < blocks:
+            score(number + 1)
+        weigh(number)
+        at, first = divmod(number, GROUPS // stack)
+        if first == GROUPS // stack - 1:
+            mine, own_head = parts[at]
+            if mine:
+                head = stage if own_head else other
+                width = GROUPS * HD
+                target = outs[0].at[doc, :, pl.ds(pl.multiple_of(head * width, width), width)]
+            else:
+                target = outs[-1]
+            finished.append(begin(results.at[at], target))
+    for copy in finished:
+        copy.wait()
+
+
+def pack_kernel(template, owner_table, place, queries, doc_keys, doc_values, where, first, rest, local, sems):
+    me, stage = place[0], place[1]
+    other = 1 - stage
+    docs, span, _ = queries.shape
+    width = GROUPS * HD
+    where[0] = stage
+    doc_at = []
+    for distance in range(docs):
+        found = jnp.int32(0)
+        for doc in range(docs):
+            found = jnp.where(owner_table[template[doc, 0]] == me ^ distance, doc, found)
+        where[distance + 1] = found
+        doc_at.append(found)
+    where[5] = jnp.where((me == 0) | (me == docs - 1), 1, 0)
+    where[6] = me
+    where[7] = other
+    columns = pl.ds(pl.multiple_of(other * width, width), width)
+    theirs, mine = head_slice(other * HD), head_slice(stage * HD)
+    copies = [
+        (queries.at[doc_at[1], :, columns], first.at[0]),
+        (queries.at[doc_at[2], :, columns], rest.at[0]),
+        (queries.at[doc_at[3], :, columns], rest.at[1]),
+    ]
+    for side, source in enumerate((doc_keys, doc_values)):
+        for doc in range(docs):
+            copies.append((source.at[doc, :, theirs], local.at[doc, side]))
+        copies.append((source.at[doc_at[0], :, mine], local.at[docs, side]))
+    copies = [pltpu.make_async_copy(a, b, sems.at[i]) for i, (a, b) in enumerate(copies)]
+    for copy in copies:
+        copy.start()
+    for copy in copies:
+        copy.wait()
+
+
+def place_kernel(where, block, _, out):
+    out[0] = block[...]
+
+
+def exchanged(queries, doc_keys, doc_values, prefix_keys, prefix_values, template, owner_table):
+    owners = lax.axis_size("pre")
+    docs, span, features = queries.shape
+    length = prefix_keys.shape[1]
+    half = length // 2
+    width = GROUPS * HD
+    bf16 = jnp.bfloat16
+
+    def over(axis, pairs):
+        return lambda block: lax.ppermute(block, axis, pairs)
+
+    near = over("pre", [(i, i ^ 1) for i in range(owners)])
+    far = over("pre", [(i, i ^ 2) for i in range(owners)])
+    middle = over("pre", [(1, 2), (2, 1)])
+    forward = over("pre", [(2, 3), (1, 0)])
+    partner = over("stg", [(0, 1), (1, 0)])
+
+    me, stage = lax.axis_index("pre"), lax.axis_index("stg")
+    cache = jnp.stack([prefix_keys[0], prefix_values[0]])
+    cache = lax.dynamic_slice_in_dim(cache, stage * HD, HD, 2)
+    far_first, far_second = far(cache[:, :half]), far(cache[:, half:])
+    near_whole = near(cache)
+
+    place = jnp.where(jnp.arange(2, dtype=jnp.int32) == 0, me, stage).astype(jnp.int32)
+    anywhere = pl.BlockSpec(memory_space=pl.ANY)
+    in_smem = pl.BlockSpec(memory_space=pltpu.SMEM)
+    in_vmem = pl.BlockSpec(memory_space=pltpu.VMEM)
+    where, first_queries, rest_queries, sent_local = pl.pallas_call(
+        pack_kernel,
+        in_specs=[in_smem, in_smem, in_smem, anywhere, anywhere, anywhere],
+        out_specs=[in_smem, in_vmem, in_vmem, in_vmem],
+        out_shape=[
+            jax.ShapeDtypeStruct((8,), jnp.int32),
+            jax.ShapeDtypeStruct((1, span, width), bf16),
+            jax.ShapeDtypeStruct((2, span, width), bf16),
+            jax.ShapeDtypeStruct((docs + 1, 2, span, HD), bf16),
+        ],
+        scratch_shapes=[pltpu.SemaphoreType.DMA((3 + 2 * (docs + 1),))],
+        cost_estimate=pl.CostEstimate(flops=0, transcendentals=0, bytes_accessed=8 * span * width * 2),
+        name="pack",
+    )(template, owner_table, place, queries, doc_keys, doc_values)
+    their_local = partner(sent_local)
+    their_first = partner(first_queries)
+    their_rest = partner(rest_queries)
+
+    cache, far_first = lax.optimization_barrier((cache, far_first))
+    middle_whole, forward_first = middle(cache), forward(far_first)
+    forward_second = forward(far_second)
+
+    answer = jax.ShapeDtypeStruct(queries.shape, bf16)
+    sent = jax.ShapeDtypeStruct((span, width), bf16)
+    keys_all = length + 2 * span
+    block = STACK * span
+
+    def call(name, slot, parts, their_queries, sent_at, caches, out, outs):
+        sets = len(parts) if slot == 0 else 1
+        plan = {
+            "slot": slot,
+            "parts": parts,
+            "their_queries": their_queries is not None,
+            "sent_at": sent_at,
+            "caches": len(caches),
+            "aliased": out is not None,
+            "outs": len(outs),
+            "extra": docs,
+        }
+        args = [queries] + ([] if their_queries is None else [their_queries])
+        args += [doc_keys, doc_values, their_local, *caches] + ([] if out is None else [out])
+        copies = len(parts) * (GROUPS + 1) + sets * 2 * (2 + min(2, len(caches)))
+        return pl.pallas_call(
+            functools.partial(attend_kernel, plan, length),
+            grid_spec=pltpu.PrefetchScalarGridSpec(
+                num_scalar_prefetch=1,
+                grid=(1,),
+                in_specs=[anywhere] * len(args),
+                out_specs=[anywhere] * len(outs),
+                scratch_shapes=[
+                    pltpu.VMEM((len(parts), GROUPS * span, HD), bf16),
+                    pltpu.VMEM((sets, keys_all, HD), bf16),
+                    pltpu.VMEM((sets, keys_all, 2 * HD), bf16),
+                    pltpu.VMEM((2, block, keys_all), jnp.float32),
+                    pltpu.VMEM((len(parts), span, width), bf16),
+                    pltpu.SemaphoreType.DMA((copies,)),
+                ],
+            ),
+            out_shape=outs,
+            input_output_aliases={} if out is None else {len(args): 0},
+            compiler_params=pltpu.CompilerParams(vmem_limit_bytes=16 << 20),
+            cost_estimate=pl.CostEstimate(
+                flops=4 * len(parts) * GROUPS * span * keys_all * HD,
+                transcendentals=len(parts) * GROUPS * span * keys_all,
+                bytes_accessed=len(parts) * 4 * (span * width + keys_all * HD),
+            ),
+            name=name,
+        )(where, *args)
+
+    theirs, mine, mine_other = (False, True), (True, True), (True, False)
+    (out,) = call("held", 0, [mine, mine_other], None, 0, (prefix_keys, prefix_values), None, [answer])
+    out, first_sent = call("near", 1, [theirs, mine], their_first, 0, (near_whole,), out, [answer, sent])
+    first_back = partner(first_sent)
+    out, second_sent = call("far", 2, [theirs, mine], their_rest, 0, (far_first, far_second), out, [answer, sent])
+    second_back = partner(second_sent)
+    last = (forward_first, forward_second, middle_whole)
+    (third_sent,) = call("last_theirs", 3, [theirs], their_rest, 1, last, None, [sent])
+    third_back = partner(third_sent)
+    (out,) = call("last_mine", 3, [mine], None, 0, last, out, [answer])
+    for slot, back in ((1, first_back), (2, second_back), (3, third_back)):
+        out = pl.pallas_call(
+            place_kernel,
+            grid_spec=pltpu.PrefetchScalarGridSpec(
+                num_scalar_prefetch=1,
+                grid=(1,),
+                in_specs=[pl.BlockSpec((span, width), lambda i, w: (0, 0)), anywhere],
+                out_specs=pl.BlockSpec((1, span, width), lambda i, w, slot=slot: (w[slot + 1], 0, 1 - w[0])),
+            ),
+            out_shape=answer,
+            input_output_aliases={2: 0},
+            cost_estimate=pl.CostEstimate(flops=0, transcendentals=0, bytes_accessed=4 * span * width),
+            name=f"place{slot}",
+        )(where, back, out)
+    return out
+
+
+def shards(queries, doc_keys, doc_values, prefix_keys, prefix_values, template, owner_table):
+    templates_all = owner_table.shape[0]
+    owners, stages, heads = lax.axis_size("pre"), lax.axis_size("stg"), KVH // lax.axis_size("tp")
+    docs, span, _ = queries.shape
+    paired = owners == docs == templates_all == 4 and stages == heads == 2
+    if paired and span == HD and prefix_keys.shape[1] % (2 * HD) == 0:
+        return exchanged(queries, doc_keys, doc_values, prefix_keys, prefix_values, template, owner_table)
+    matches = template == jnp.arange(templates_all, dtype=jnp.int32)[None, :]
+    holders = jnp.sum(jnp.where(matches, owner_table[None, :], 0), axis=1)
+    return gathered(queries, doc_keys, doc_values, prefix_keys, prefix_values, holders)
+
+
 def solution(mesh):
     return jax.shard_map(
         shards,

time: 163 us -> 77 us (0.47)
  the two profiles are of different devices: /device:TPU:0 before, /device:TPU:16 now
where the time goes in v2:
time: 77 us; the launch traced here: 76.6 us
  Pallas kernels  36.2 us (47%)
  starting transfers between devices  24.4 us (32%)
  waiting for transfers between devices  10.2 us (13%)
  local copies, waits for them, and re-layouts  4.01 us (5%)
  other arithmetic  1.65 us (2%)
    pallas_call x5, Pallas kernels, call(): pl.pallas_call(functools.partial(attend_kernel, plan, length), grid_spec=...  26.2 us
    ppermute x12, starting transfers between devices, over(): return lambda block: lax.ppermute(block, axis, pairs)  24.4 us
    ppermute x12, waiting for transfers between devices, over(): return lambda block: lax.ppermute(block, axis, pairs)  10.2 us
    pallas_call x3, Pallas kernels, exchanged(): pl.pallas_call(place_kernel, grid_spec=pltpu.PrefetchScalarGridSpec(num_s...  6.99 us
    unnamed x19, local copies, waits for them, and re-layouts  3.2 us
    pallas_call x1, Pallas kernels, exchanged(): pl.pallas_call(pack_kernel, in_specs=[in_smem, in_smem, in_smem, anywhere...  3.02 us
  transfers between devices with their start and end apart: 12, of which 2 were waited for; matrix products, arithmetic and copies ran while one was open for 2% of the time, Pallas kernels for 44%

profile of v2, /device:TPU:16, one launch (start us, length us, event | category | flops | bytes accessed | tf_op | source)
XLA Modules:
  0.0 76.6 jit_solution(5549199537079331888)
XLA Ops:
  0.0 1.1 %fusion = bf16[2,1024,128]{2,1,0:T(8,128)(2,1)S(1)} fusion(s32[]{:T(128)S(6)} %select_n.8, bf16[1,1024,256]{2,1,0:T(8,128)(2,1)} %refs_3_.1, bf16[1,1024,256]{2,1,0:T(8,128)(2,1)} %refs_4_.1), kind=kLoop, calls=%fused_computation.2 | loop fusion | flops 1048576 | bytes 1572868 | tf_op jit(solution)/shard_map/stack | solution.py:287
  1.1 0.0 copy-start.6
  1.1 0.0 copy-start
  1.1 0.0 copy-start.1
  1.1 0.0 copy-start.2
  1.1 0.0 copy-start.3
  1.1 0.8 %fusion.1 = (bf16[2,512,128]{2,1,0:T(8,128)(2,1)}, bf16[2,512,128]{2,1,0:T(8,128)(2,1)}) fusion(bf16[2,1024,128]{2,1,0:T(8,128)(2,1)S(1)} %fusion), kind=kLoop, calls=%fused_computation.4 | loop fusion | bytes 1048576 | tf_op jit(solution)/shard_map/slice | solution.py:289
  2.0 0.1 copy-done.6
  2.1 0.0 collective-permute-start.2
  2.1 0.0 copy-done.8
  2.1 0.7 copy.14.template
  2.7 0.6 compare_select_fusion.place
  3.3 3.0 %pack.1 = (s32[8]{0:T(128)}, bf16[1,128,1024]{2,1,0:T(8,128)(2,1)}, bf16[2,128,1024]{2,1,0:T(8,128)(2,1)}, bf16[5,2,128,128]{3,2,1,0:T(8,128)(2,1)}) custom-call(s32[4,1]{1,0:T(4,128)} %copy.14.template, s32[4]{0:T(128)} %owner_table.1, s32[2]{0:T(128)} %compare_select_fusion.place, bf16[4,128,2048]{2,1,0:T(8,128)(2,1)} %queries.11, ...), custom_call_target="tpu_custom_call" | custom-call | bytes 2097152 | tf_op jit(solution)/shard_map/pack/pallas_call | solution.py:296
  6.3 1.8 %collective-permute-start.8 = (bf16[1,128,1024]{2,1,0:T(8,128)(2,1)}, bf16[1,128,1024]{2,1,0:T(8,128)(2,1)S(1)}, u32[]{:S(2)}, u32[]{:S(2)}) collective-permute-start(bf16[1,128,1024]{2,1,0:T(8,128)(2,1)} %get-tuple-element.20), channel_id=1, source_target_pairs={{0,2},{2,0},{1,3},{3,1},{4,6},{6,4},{5,7},{7,5},{8,10},{10,8},{9,1... | collective-permute-start | bytes 786440 | tf_op jit(solution)/shard_map/ppermute | solution.py:278
  8.2 1.6 %collective-permute-start.9 = (bf16[2,1024,128]{2,1,0:T(8,128)(2,1)}, bf16[2,1024,128]{2,1,0:T(8,128)(2,1)S(1)}, u32[]{:S(2)}, u32[]{:S(2)}) collective-permute-start(bf16[2,1024,128]{2,1,0:T(8,128)(2,1)} %copy-done.6), channel_id=1, source_target_pairs={{0,4},{4,0},{8,12},{12,8},{1,5},{5,1},{9,13},{13,9},{2,6},{6,2},{1... | collective-permute-start | bytes 1572872 | tf_op jit(solution)/shard_map/ppermute | solution.py:278
  9.8 0.6 collective-permute-start.1
  10.3 1.4 %collective-permute-start = (bf16[2,128,1024]{2,1,0:T(8,128)(2,1)}, bf16[2,128,1024]{2,1,0:T(8,128)(2,1)S(1)}, u32[]{:S(2)}, u32[]{:S(2)}) collective-permute-start(bf16[2,128,1024]{2,1,0:T(8,128)(2,1)} %get-tuple-element.16), channel_id=1, source_target_pairs={{0,2},{2,0},{1,3},{3,1},{4,6},{6,4},{5,7},{7,5},{8,10},{10,8},{9,1... | collective-permute-start | bytes 1572872 | tf_op jit(solution)/shard_map/ppermute | solution.py:278
  11.8 2.1 %collective-permute-done.2.refs_4_ = bf16[2,512,128]{2,1,0:T(8,128)(2,1)S(1)} collective-permute-done((bf16[2,512,128]{2,1,0:T(8,128)(2,1)}, bf16[2,512,128]{2,1,0:T(8,128)(2,1)S(1)}, u32[]{:S(2)}, u32[]{:S(2)}) %collective-permute-start.2) | collective-permute-done | bytes 262176 | tf_op jit(solution)/shard_map/ppermute | solution.py:278
  13.9 3.3 %collective-permute-start.4 = (bf16[2,512,128]{2,1,0:T(8,128)(2,1)}, bf16[2,512,128]{2,1,0:T(8,128)(2,1)S(1)}, u32[]{:S(2)}, u32[]{:S(2)}) collective-permute-start(bf16[2,512,128]{2,1,0:T(8,128)(2,1)} %get-tuple-element.25), channel_id=1, source_target_pairs={{0,8},{4,12},{8,0},{12,4},{1,9},{5,13},{9,1},{13,5},{2,10},{6,14},... | collective-permute-start | bytes 786440 | tf_op jit(solution)/shard_map/ppermute | solution.py:278
  17.2 0.0 collective-permute-done.8.refs_0_
  17.2 4.5 %collective-permute-start.6 = (bf16[2,1024,128]{2,1,0:T(8,128)(2,1)}, bf16[2,1024,128]{2,1,0:T(8,128)(2,1)S(1)}, u32[]{:S(2)}, u32[]{:S(2)}) collective-permute-start(bf16[2,1024,128]{2,1,0:T(8,128)(2,1)} %copy-done.6), channel_id=1, source_target_pairs={{4,8},{8,4},{5,9},{9,5},{6,10},{10,6},{7,11},{11,7},{20,24},{24,20... | collective-permute-start | bytes 1572872 | tf_op jit(solution)/shard_map/ppermute | solution.py:278
  21.8 8.1 %collective-permute-done.4.refs_5_ = bf16[2,512,128]{2,1,0:T(8,128)(2,1)S(1)} collective-permute-done((bf16[2,512,128]{2,1,0:T(8,128)(2,1)}, bf16[2,512,128]{2,1,0:T(8,128)(2,1)S(1)}, u32[]{:S(2)}, u32[]{:S(2)}) %collective-permute-start.4) | collective-permute-done | bytes 262176 | tf_op jit(solution)/shard_map/ppermute | solution.py:278
  29.8 6.4 %collective-permute-start.3 = (bf16[2,512,128]{2,1,0:T(8,128)(2,1)S(1)}, bf16[2,512,128]{2,1,0:T(8,128)(2,1)S(1)}, u32[]{:S(2)}, u32[]{:S(2)}) collective-permute-start(bf16[2,512,128]{2,1,0:T(8,128)(2,1)S(1)} %collective-permute-done.2.refs_4_), channel_id=1, source_target_pairs={{8,12},{4,0},{9,13},{5,1},{10,14},{6,2},{11,15},{7,3},{24,28},{20,... | collective-permute-start | bytes 786440 | tf_op jit(solution)/shard_map/ppermute | solution.py:278
  36.3 0.0 collective-permute-done.1.refs_3_.refs_2_
  36.3 1.3 %collective-permute-start.5 = (bf16[2,512,128]{2,1,0:T(8,128)(2,1)S(1)}, bf16[2,512,128]{2,1,0:T(8,128)(2,1)S(1)}, u32[]{:S(2)}, u32[]{:S(2)}) collective-permute-start(bf16[2,512,128]{2,1,0:T(8,128)(2,1)S(1)} %collective-permute-done.4.refs_5_), channel_id=1, source_target_pairs={{8,12},{4,0},{9,13},{5,1},{10,14},{6,2},{11,15},{7,3},{24,28},{20,... | collective-permute-start | bytes 786440 | tf_op jit(solution)/shard_map/ppermute | solution.py:278
  37.6 0.0 copy-start.4
  37.6 1.0 %copy-done.4 = bf16[1,1024,256]{2,1,0:T(8,128)(2,1)S(1)} copy-done((bf16[1,1024,256]{2,1,0:T(8,128)(2,1)S(1)}, bf16[1,1024,256]{2,1,0:T(8,128)(2,1)}, u32[]{:S(2)}) %copy-start.4) | copy-done | bytes 524312
  38.7 0.7 copy-done.5
  39.3 6.3 %held.1.refs_5_ = bf16[4,128,2048]{2,1,0:T(8,128)(2,1)} custom-call(s32[8]{0:T(128)S(1)} %copy-done.5, bf16[4,128,2048]{2,1,0:T(8,128)(2,1)S(1)} %copy-done, bf16[4,128,256]{2,1,0:T(8,128)(2,1)S(1)} %copy-done.1, bf16[4,128,256]{2,1,0:T(8,128)(2,1)S(1)} %copy-done.2, bf16[5,2,128,128]{3,2,1,0:T(8,128)(2,1)S(1)} %collective-permute-done.1.refs_3_.refs_2_, ...), custom_call_target="tpu_custom_call" | custom-call | flops 1342177280 | bytes 2359296 | tf_op jit(solution)/shard_map/held/pallas_call | solution.py:338
  45.7 0.0 collective-permute-done.9.refs_4_
  45.7 6.0 %near.1 = (bf16[4,128,2048]{2,1,0:T(8,128)(2,1)}, bf16[128,1024]{1,0:T(8,128)(2,1)S(1)}) custom-call(s32[8]{0:T(128)S(1)} %copy-done.5, bf16[4,128,2048]{2,1,0:T(8,128)(2,1)S(1)} %copy-done, bf16[1,128,1024]{2,1,0:T(8,128)(2,1)S(1)} %collective-permute-done.8.refs_0_, bf16[4,128,256]{2,1,0:T(8,128)(2,1)S(1)} %copy-done.1, ...), custom_call_target="tpu_custom_call", output_to_operand_aliasing={{0}: (7, {})} | custom-call | flops 1342177280 | bytes 2359296 | tf_op jit(solution)/shard_map/near/pallas_call | solution.py:338
  51.7 1.2 %collective-permute-start.11 = (bf16[128,1024]{1,0:T(8,128)(2,1)S(1)}, bf16[128,1024]{1,0:T(8,128)(2,1)S(1)}, u32[]{:S(2)}, u32[]{:S(2)}) collective-permute-start(bf16[128,1024]{1,0:T(8,128)(2,1)S(1)} %get-tuple-element.23), channel_id=1, source_target_pairs={{0,2},{2,0},{1,3},{3,1},{4,6},{6,4},{5,7},{7,5},{8,10},{10,8},{9,1... | collective-permute-start | bytes 786440 | tf_op jit(solution)/shard_map/ppermute | solution.py:278
  52.9 0.0 collective-permute-done.refs_0_
  52.9 6.5 %far.1 = (bf16[4,128,2048]{2,1,0:T(8,128)(2,1)}, bf16[128,1024]{1,0:T(8,128)(2,1)S(1)}) custom-call(s32[8]{0:T(128)S(1)} %copy-done.5, bf16[4,128,2048]{2,1,0:T(8,128)(2,1)S(1)} %copy-done, bf16[2,128,1024]{2,1,0:T(8,128)(2,1)S(1)} %collective-permute-done.refs_0_, bf16[4,128,256]{2,1,0:T(8,128)(2,1)S(1)} %copy-done.1, ...), custom_call_target="tpu_custom_call", output_to_operand_aliasing={{0}: (8, {})} | custom-call | flops 1342177280 | bytes 2359296 | tf_op jit(solution)/shard_map/far/pallas_call | solution.py:338
  59.4 1.0 %collective-permute-start.10 = (bf16[128,1024]{1,0:T(8,128)(2,1)S(1)}, bf16[128,1024]{1,0:T(8,128)(2,1)}, u32[]{:S(2)}, u32[]{:S(2)}) collective-permute-start(bf16[128,1024]{1,0:T(8,128)(2,1)S(1)} %get-tuple-element.22), channel_id=1, source_target_pairs={{0,2},{2,0},{1,3},{3,1},{4,6},{6,4},{5,7},{7,5},{8,10},{10,8},{9,1... | collective-permute-start | bytes 786440 | tf_op jit(solution)/shard_map/ppermute | solution.py:278
  60.4 0.0 collective-permute-done.3.refs_4_.refs_3_
  60.4 0.0 collective-permute-done.5.refs_5_.refs_4_
  60.4 0.0 collective-permute-done.6.refs_6_.refs_5_
  60.4 3.3 %last_theirs.1 = bf16[128,1024]{1,0:T(8,128)(2,1)S(1)} custom-call(s32[8]{0:T(128)S(1)} %copy-done.5, bf16[4,128,2048]{2,1,0:T(8,128)(2,1)S(1)} %copy-done, bf16[2,128,1024]{2,1,0:T(8,128)(2,1)S(1)} %collective-permute-done.refs_0_, bf16[4,128,256]{2,1,0:T(8,128)(2,1)S(1)} %copy-done.1, bf16[4,128,256]{2,1,0:T(8,128)(2,1)S(1)} %copy-done.2, ...), custom_call_target="tpu_custom_call" | custom-call | flops 671088640 | bytes 1179648 | tf_op jit(solution)/shard_map/last_theirs/pallas_call | solution.py:338
  63.7 1.2 %collective-permute-start.7 = (bf16[128,1024]{1,0:T(8,128)(2,1)S(1)}, bf16[128,1024]{1,0:T(8,128)(2,1)}, u32[]{:S(2)}, u32[]{:S(2)}) collective-permute-start(bf16[128,1024]{1,0:T(8,128)(2,1)S(1)} %last_theirs.1), channel_id=1, source_target_pairs={{0,2},{2,0},{1,3},{3,1},{4,6},{6,4},{5,7},{7,5},{8,10},{10,8},{9,1... | collective-permute-start | bytes 786440 | tf_op jit(solution)/shard_map/ppermute | solution.py:278
  64.9 4.0 %last_mine.1._ = bf16[4,128,2048]{2,1,0:T(8,128)(2,1)} custom-call(s32[8]{0:T(128)S(1)} %copy-done.5, bf16[4,128,2048]{2,1,0:T(8,128)(2,1)S(1)} %copy-done, bf16[4,128,256]{2,1,0:T(8,128)(2,1)S(1)} %copy-done.1, bf16[4,128,256]{2,1,0:T(8,128)(2,1)S(1)} %copy-done.2, ...), custom_call_target="tpu_custom_call", output_to_operand_aliasing={{}: (8, {})} | custom-call | flops 671088640 | bytes 1179648 | tf_op jit(solution)/shard_map/last_mine/pallas_call | solution.py:338
  68.9 0.0 collective-permute-done.11.block
  68.9 0.7 copy-done.7
  69.6 2.3 %place1.1._ = bf16[4,128,2048]{2,1,0:T(8,128)(2,1)} custom-call(s32[8]{0:T(128)} %get-tuple-element.15.where, bf16[128,1024]{1,0:T(8,128)(2,1)} %copy-done.7, bf16[4,128,2048]{2,1,0:T(8,128)(2,1)} %last_mine.1._), custom_call_target="tpu_custom_call", output_to_operand_aliasing={{}: (2, {})} | custom-call | bytes 524288 | tf_op jit(solution)/shard_map/place1/pallas_call | solution.py:376
  71.9 0.0 collective-permute-done.10.block
  71.9 2.3 %place2.1._ = bf16[4,128,2048]{2,1,0:T(8,128)(2,1)} custom-call(s32[8]{0:T(128)} %get-tuple-element.15.where, bf16[128,1024]{1,0:T(8,128)(2,1)} %collective-permute-done.10.block, bf16[4,128,2048]{2,1,0:T(8,128)(2,1)} %place1.1._), custom_call_target="tpu_custom_call", output_to_operand_aliasing={{}: (2, {})} | custom-call | bytes 524288 | tf_op jit(solution)/shard_map/place2/pallas_call | solution.py:376
  74.3 0.0 collective-permute-done.7.block
  74.3 2.3 %place3.1 = bf16[4,128,2048]{2,1,0:T(8,128)(2,1)} custom-call(s32[8]{0:T(128)} %get-tuple-element.15.where, bf16[128,1024]{1,0:T(8,128)(2,1)} %collective-permute-done.7.block, bf16[4,128,2048]{2,1,0:T(8,128)(2,1)} %place2.1._), custom_call_target="tpu_custom_call", output_to_operand_aliasing={{}: (2, {})} | custom-call | bytes 524288 | tf_op jit(solution)/shard_map/place3/pallas_call | solution.py:376
  (7 shorter events, 0.0 us)
Async XLA Ops:
  0.0 2.1 %copy-start.8 = (s32[4,1]{0,1:T(1,128)S(1)}, s32[4,1]{0,1:T(1,128)}, u32[]{:S(2)}) copy-start(s32[4,1]{0,1:T(1,128)} %param.12) | copy-start | bytes 52
  1.1 1.0 %copy-start.6 = (bf16[2,1024,128]{2,1,0:T(8,128)(2,1)}, bf16[2,1024,128]{2,1,0:T(8,128)(2,1)S(1)}, u32[]{:S(2)}) copy-start(bf16[2,1024,128]{2,1,0:T(8,128)(2,1)S(1)} %fusion) | copy-start | bytes 1572868
  1.1 36.5 %copy-start = (bf16[4,128,2048]{2,1,0:T(8,128)(2,1)S(1)}, bf16[4,128,2048]{2,1,0:T(8,128)(2,1)}, u32[]{:S(2)}) copy-start(bf16[4,128,2048]{2,1,0:T(8,128)(2,1)} %queries.11) | copy-start | bytes 6291460
  1.1 36.5 %copy-start.1 = (bf16[4,128,256]{2,1,0:T(8,128)(2,1)S(1)}, bf16[4,128,256]{2,1,0:T(8,128)(2,1)}, u32[]{:S(2)}) copy-start(bf16[4,128,256]{2,1,0:T(8,128)(2,1)} %refs_0_.3) | copy-start | bytes 786436
  1.1 36.5 %copy-start.2 = (bf16[4,128,256]{2,1,0:T(8,128)(2,1)S(1)}, bf16[4,128,256]{2,1,0:T(8,128)(2,1)}, u32[]{:S(2)}) copy-start(bf16[4,128,256]{2,1,0:T(8,128)(2,1)} %refs_1_.9) | copy-start | bytes 786436
  1.1 36.5 %copy-start.3 = (bf16[1,1024,256]{2,1,0:T(8,128)(2,1)S(1)}, bf16[1,1024,256]{2,1,0:T(8,128)(2,1)}, u32[]{:S(2)}) copy-start(bf16[1,1024,256]{2,1,0:T(8,128)(2,1)} %refs_3_.1) | copy-start | bytes 1572868
  2.1 11.8 %collective-permute-start.2 = (bf16[2,512,128]{2,1,0:T(8,128)(2,1)}, bf16[2,512,128]{2,1,0:T(8,128)(2,1)S(1)}, u32[]{:S(2)}, u32[]{:S(2)}) collective-permute-start(bf16[2,512,128]{2,1,0:T(8,128)(2,1)} %get-tuple-element.26), channel_id=1, source_target_pairs={{0,8},{4,12},{8,0},{12,4},{1,9},{5,13},{9,1},{13,5},{2,10},{6,14},... | collective-permute-start | bytes 786440 | tf_op jit(solution)/shard_map/ppermute | solution.py:278
  6.3 10.9 %collective-permute-start.8 = (bf16[1,128,1024]{2,1,0:T(8,128)(2,1)}, bf16[1,128,1024]{2,1,0:T(8,128)(2,1)S(1)}, u32[]{:S(2)}, u32[]{:S(2)}) collective-permute-start(bf16[1,128,1024]{2,1,0:T(8,128)(2,1)} %get-tuple-element.20), channel_id=1, source_target_pairs={{0,2},{2,0},{1,3},{3,1},{4,6},{6,4},{5,7},{7,5},{8,10},{10,8},{9,1... | collective-permute-start | bytes 786440 | tf_op jit(solution)/shard_map/ppermute | solution.py:278
  8.2 37.5 %collective-permute-start.9 = (bf16[2,1024,128]{2,1,0:T(8,128)(2,1)}, bf16[2,1024,128]{2,1,0:T(8,128)(2,1)S(1)}, u32[]{:S(2)}, u32[]{:S(2)}) collective-permute-start(bf16[2,1024,128]{2,1,0:T(8,128)(2,1)} %copy-done.6), channel_id=1, source_target_pairs={{0,4},{4,0},{8,12},{12,8},{1,5},{5,1},{9,13},{13,9},{2,6},{6,2},{1... | collective-permute-start | bytes 1572872 | tf_op jit(solution)/shard_map/ppermute | solution.py:278
  9.8 26.5 %collective-permute-start.1 = (bf16[5,2,128,128]{3,2,1,0:T(8,128)(2,1)}, bf16[5,2,128,128]{3,2,1,0:T(8,128)(2,1)S(1)}, u32[]{:S(2)}, u32[]{:S(2)}) collective-permute-start(bf16[5,2,128,128]{3,2,1,0:T(8,128)(2,1)} %get-tuple-element.17), channel_id=1, source_target_pairs={{0,2},{2,0},{1,3},{3,1},{4,6},{6,4},{5,7},{7,5},{8,10},{10,8},{9,1... | collective-permute-start | bytes 983048 | tf_op jit(solution)/shard_map/ppermute | solution.py:278
  10.3 42.6 %collective-permute-start = (bf16[2,128,1024]{2,1,0:T(8,128)(2,1)}, bf16[2,128,1024]{2,1,0:T(8,128)(2,1)S(1)}, u32[]{:S(2)}, u32[]{:S(2)}) collective-permute-start(bf16[2,128,1024]{2,1,0:T(8,128)(2,1)} %get-tuple-element.16), channel_id=1, source_target_pairs={{0,2},{2,0},{1,3},{3,1},{4,6},{6,4},{5,7},{7,5},{8,10},{10,8},{9,1... | collective-permute-start | bytes 1572872 | tf_op jit(solution)/shard_map/ppermute | solution.py:278
  13.9 16.0 %collective-permute-start.4 = (bf16[2,512,128]{2,1,0:T(8,128)(2,1)}, bf16[2,512,128]{2,1,0:T(8,128)(2,1)S(1)}, u32[]{:S(2)}, u32[]{:S(2)}) collective-permute-start(bf16[2,512,128]{2,1,0:T(8,128)(2,1)} %get-tuple-element.25), channel_id=1, source_target_pairs={{0,8},{4,12},{8,0},{12,4},{1,9},{5,13},{9,1},{13,5},{2,10},{6,14},... | collective-permute-start | bytes 786440 | tf_op jit(solution)/shard_map/ppermute | solution.py:278
  17.2 43.2 %collective-permute-start.6 = (bf16[2,1024,128]{2,1,0:T(8,128)(2,1)}, bf16[2,1024,128]{2,1,0:T(8,128)(2,1)S(1)}, u32[]{:S(2)}, u32[]{:S(2)}) collective-permute-start(bf16[2,1024,128]{2,1,0:T(8,128)(2,1)} %copy-done.6), channel_id=1, source_target_pairs={{4,8},{8,4},{5,9},{9,5},{6,10},{10,6},{7,11},{11,7},{20,24},{24,20... | collective-permute-start | bytes 1572872 | tf_op jit(solution)/shard_map/ppermute | solution.py:278
  29.8 30.6 %collective-permute-start.3 = (bf16[2,512,128]{2,1,0:T(8,128)(2,1)S(1)}, bf16[2,512,128]{2,1,0:T(8,128)(2,1)S(1)}, u32[]{:S(2)}, u32[]{:S(2)}) collective-permute-start(bf16[2,512,128]{2,1,0:T(8,128)(2,1)S(1)} %collective-permute-done.2.refs_4_), channel_id=1, source_target_pairs={{8,12},{4,0},{9,13},{5,1},{10,14},{6,2},{11,15},{7,3},{24,28},{20,... | collective-permute-start | bytes 786440 | tf_op jit(solution)/shard_map/ppermute | solution.py:278
  36.3 24.1 %collective-permute-start.5 = (bf16[2,512,128]{2,1,0:T(8,128)(2,1)S(1)}, bf16[2,512,128]{2,1,0:T(8,128)(2,1)S(1)}, u32[]{:S(2)}, u32[]{:S(2)}) collective-permute-start(bf16[2,512,128]{2,1,0:T(8,128)(2,1)S(1)} %collective-permute-done.4.refs_5_), channel_id=1, source_target_pairs={{8,12},{4,0},{9,13},{5,1},{10,14},{6,2},{11,15},{7,3},{24,28},{20,... | collective-permute-start | bytes 786440 | tf_op jit(solution)/shard_map/ppermute | solution.py:278
  37.6 1.0 %copy-start.4 = (bf16[1,1024,256]{2,1,0:T(8,128)(2,1)S(1)}, bf16[1,1024,256]{2,1,0:T(8,128)(2,1)}, u32[]{:S(2)}) copy-start(bf16[1,1024,256]{2,1,0:T(8,128)(2,1)} %refs_4_.1) | copy-start | bytes 1572868
  38.7 0.7 copy-start.5
  51.7 17.2 %collective-permute-start.11 = (bf16[128,1024]{1,0:T(8,128)(2,1)S(1)}, bf16[128,1024]{1,0:T(8,128)(2,1)S(1)}, u32[]{:S(2)}, u32[]{:S(2)}) collective-permute-start(bf16[128,1024]{1,0:T(8,128)(2,1)S(1)} %get-tuple-element.23), channel_id=1, source_target_pairs={{0,2},{2,0},{1,3},{3,1},{4,6},{6,4},{5,7},{7,5},{8,10},{10,8},{9,1... | collective-permute-start | bytes 786440 | tf_op jit(solution)/shard_map/ppermute | solution.py:278
  59.4 12.5 %collective-permute-start.10 = (bf16[128,1024]{1,0:T(8,128)(2,1)S(1)}, bf16[128,1024]{1,0:T(8,128)(2,1)}, u32[]{:S(2)}, u32[]{:S(2)}) collective-permute-start(bf16[128,1024]{1,0:T(8,128)(2,1)S(1)} %get-tuple-element.22), channel_id=1, source_target_pairs={{0,2},{2,0},{1,3},{3,1},{4,6},{6,4},{5,7},{7,5},{8,10},{10,8},{9,1... | collective-permute-start | bytes 786440 | tf_op jit(solution)/shard_map/ppermute | solution.py:278
  63.7 10.6 %collective-permute-start.7 = (bf16[128,1024]{1,0:T(8,128)(2,1)S(1)}, bf16[128,1024]{1,0:T(8,128)(2,1)}, u32[]{:S(2)}, u32[]{:S(2)}) collective-permute-start(bf16[128,1024]{1,0:T(8,128)(2,1)S(1)} %last_theirs.1), channel_id=1, source_target_pairs={{0,2},{2,0},{1,3},{3,1},{4,6},{6,4},{5,7},{7,5},{8,10},{10,8},{9,1... | collective-permute-start | bytes 786440 | tf_op jit(solution)/shard_map/ppermute | solution.py:278
  68.9 0.7 copy-start.7
